TPU v7x, 256 devices: a whole 4x4x8 slice. The times are simulated.
256 devices in a mesh: half: 2 (over y_lo), shard: 128 (over y_hi, z, x, core).
Axes of the slice: x: 4, y: 4 (y_hi: 2, y_lo: 2; y = y_hi * 2 + y_lo), z: 8, core: 2. Of those that a mesh axis runs over, the one named last changes fastest.
Arguments:
- recording: float32 [32, 2048, 1024], P('half', 'shard'), may hold values from -600 to 600
- source_channels: int32 [256], replicated, may hold values from 0 to 2047, as said below
Outputs:
- correlations: float32 [256, 2048, 512], P('half', 'shard')
Inputs may be any that keep to these rules, and one draw needn't show every extreme that they name: `source_channels`: distinct channel indices.
All inputs are finite; a program needn't handle non-finite values.
Results may differ from a plain program's by a relative error of at most 0.000071.
Values sent between devices are 32-bit elements; how exact they have to be, the bound alone decides.
A program may use at most 64 MiB of HBM per device.

v0:
```python
import jax
import jax.numpy as jnp
from jax import lax
from jax.sharding import PartitionSpec as P

F = 128
LAGS = 512
SMOOTH = 2
SEG = 32


water_level = 0.2
epsilon = 1e-05


def partner_2(x, axis, bit):
    return lax.ppermute(x, axis, [(i, i ^ 1 << bit) for i in range(lax.axis_size(axis))])


def forward_table(samples, freq_count):
    bins = jnp.arange(freq_count, dtype=jnp.int32) + 1
    times = jnp.arange(samples, dtype=jnp.int32)
    phase = bins[:, None] * times[None, :] % samples
    angle = 2.0 * jnp.pi * phase.astype(jnp.float32) / samples
    taper = 0.5 - 0.5 * jnp.cos(2.0 * jnp.pi * times.astype(jnp.float32) / samples)
    return jnp.stack((jnp.cos(angle) * taper[None, :], -jnp.sin(angle) * taper[None, :]), axis=1)


def inverse_table(samples, freq_count, lag_count, segments):
    bins = jnp.arange(freq_count, dtype=jnp.int32) + 1
    shifts = jnp.arange(lag_count, dtype=jnp.int32) - lag_count // 2
    phase = bins[:, None] * shifts[None, :] % samples
    angle = 2.0 * jnp.pi * phase.astype(jnp.float32) / samples
    scale = 1.0 / jnp.sqrt(jnp.float32(segments * freq_count))
    return jnp.stack((jnp.cos(angle) * scale, -jnp.sin(angle) * scale), axis=1)


def whiten(spectra):
    magnitude = jnp.sqrt(spectra[:, 0] * spectra[:, 0] + spectra[:, 1] * spectra[:, 1])
    freq_count = magnitude.shape[0]
    padded = jnp.pad(magnitude, ((SMOOTH, SMOOTH), (0, 0), (0, 0)))
    smoothed = padded[0:freq_count]
    for offset in range(1, 2 * SMOOTH + 1):
        smoothed = smoothed + padded[offset : offset + freq_count]
    smoothed = smoothed / (2 * SMOOTH + 1)
    water_mark = jnp.mean(magnitude, axis=0, keepdims=True)
    divisor = smoothed + water_level * water_mark + epsilon
    return spectra / divisor[:, None]


def correlate(whitened, indices):
    sources = jnp.take(whitened, indices, axis=2)
    src_real, src_imag = (sources[:, 0], sources[:, 1])
    rec_real, rec_imag = (whitened[:, 0], whitened[:, 1])
    high = lax.Precision.HIGHEST
    cross_real = jnp.einsum("fnx,fcx->fnc", src_real, rec_real, precision=high) + jnp.einsum(
        "fnx,fcx->fnc", src_imag, rec_imag, precision=high
    )
    cross_imag = jnp.einsum("fnx,fcx->fnc", src_real, rec_imag, precision=high) - jnp.einsum(
        "fnx,fcx->fnc", src_imag, rec_real, precision=high
    )
    return jnp.stack((cross_real, cross_imag), axis=1)


def body(recording, source_channels):
    samples = recording.shape[2]
    forward = forward_table(samples, F)
    spectra = jnp.einsum("fqt,sct->fqcs", forward, recording, precision=lax.Precision.HIGHEST)
    whitened = whiten(spectra)
    by_freq = lax.all_to_all(whitened, "shard", split_axis=0, concat_axis=2, tiled=True)
    per_half = source_channels.shape[0] // lax.axis_size("half")
    half_index = lax.axis_index("half")
    own_sources = lax.dynamic_slice_in_dim(source_channels, half_index * per_half, per_half)
    partner = partner_2(by_freq, "half", 0)
    combined = jnp.concatenate((by_freq, partner), axis=3)
    cross = correlate(combined, own_sources)
    backward = inverse_table(samples, F, LAGS, SEG)
    return jnp.einsum(
        "fqnc,fql->ncl",
        lax.all_to_all(cross, "shard", split_axis=3, concat_axis=0, tiled=True),
        backward,
        precision=lax.Precision.HIGHEST,
    )


def solution(mesh):
    return jax.shard_map(
        body,
        mesh=mesh,
        in_specs=(P("half", "shard", None), P()),
        out_specs=P("half", "shard", None),
        check_vma=False,
    )
```

profile of v0, /device:TPU:1, one launch (start us, length us, event | category | flops | bytes accessed | tf_op | source)
XLA Modules:
  0.0 138.3 jit_solution(13106528990922026452)
XLA Ops:
  0.0 0.0 copy-start
  0.1 2.2 %cosine_multiply_fusion = (f32[128,1,1024]{2,0,1:T(8,128)S(1)}, f32[128,1,1024]{2,0,1:T(8,128)S(1)}) fusion(f32[1024]{0:T(1024)S(1)} %multiply_subtract_fusion, s32[128]{0:T(128)S(1)} %iota_add_fusion.1), kind=kLoop, calls=%fused_computation.23 | loop fusion | flops 2228224 | bytes 1053184 | tf_op jit(solution)/shard_map/mul | solution.py:26
  2.2 0.0 copy-done
  2.2 1.0 convolution_bitcast_fusion.1
  3.3 0.1 fusion.28
  3.4 0.2 fusion.25
  3.7 0.0 copy-start.1
  3.7 1.8 %copy.11 = f32[128,2,16,16]{2,3,1,0:T(8,128)S(1)} copy(f32[128,2,16,16]{0,2,3,1:T(8,128)S(1)} %broadcast_divide_fusion) | data formatting | bytes 524288 | tf_op jit(solution)/shard_map/div | solution.py:48
  5.5 1.5 %reshape.356 = f32[128,1,512]{2,1,0:T(1,128)} reshape(f32[128,2,16,16]{3,2,1,0:T(8,128)S(1)} %bitcast.58) | data formatting | bytes 524288
  7.0 16.4 %all-to-all-start = ((f32[128,1,512]{2,1,0:T(1,128)}), f32[128,1,512]{2,1,0:T(1,128)S(1)}, u32[]{:S(2)}, u32[]{:S(2)}) async-start(f32[128,1,512]{2,1,0:T(1,128)} %reshape.356), calls=%async_computation | async-start | bytes 524288 | tf_op jit(solution)/shard_map/all_to_all | solution.py:70
  23.4 0.0 copy-done.1
  23.4 0.1 compare_and_fusion
  23.5 16.5 %all-to-all-done = f32[128,1,512]{2,1,0:T(1,128)S(1)} async-done(((f32[128,1,512]{2,1,0:T(1,128)}), f32[128,1,512]{2,1,0:T(1,128)S(1)}, u32[]{:S(2)}, u32[]{:S(2)}) %all-to-all-start) | async-done | bytes 262176 | tf_op jit(solution)/shard_map/all_to_all | solution.py:70
  40.0 0.5 broadcast.371
  40.5 1.3 reduce.1
  41.7 0.7 reshape.357
  42.5 0.2 bitcast_bitcast_fusion
  42.6 1.2 copy.12
  43.9 1.6 %all_to_all.29 = f32[1,2,2048,16]{2,3,1,0:T(8,128)S(1)} reshape(f32[1,2,128,16,16]{3,2,4,1,0:T(8,128)S(1)} %copy.12) | data formatting | bytes 524288 | tf_op jit(solution)/shard_map/all_to_all | solution.py:70
  45.4 0.5 collective-permute-start
  45.9 7.0 %collective-permute-done = f32[1,2,2048,16]{2,3,1,0:T(8,128)S(1)} collective-permute-done((f32[1,2,2048,16]{2,3,1,0:T(8,128)S(1)}, f32[1,2,2048,16]{2,3,1,0:T(8,128)S(1)}, u32[]{:S(2)}, u32[]{:S(2)}) %collective-permute-start) | collective-permute-done | bytes 262176 | tf_op jit(solution)/shard_map/ppermute | solution.py:17
  53.0 2.3 %copy.13 = f32[1,2,2048,32]{3,1,2,0:T(2,128)} copy(f32[1,2,2048,32]{2,3,1,0:T(8,128)S(1)} %constant_dynamic-update-slice_fusion) | data formatting | bytes 1048576 | tf_op jit(solution)/shard_map/concatenate | solution.py:75
  55.2 2.3 %gather_fusion = f32[128,2,32]{2,1,0:T(2,128)S(1)} fusion(f32[2,2048,32]{2,0,1:T(2,128)} %bitcast.60, s32[1024]{0:T(1024)S(1)} %pad_clamp_fusion), kind=kCustom, calls=%fused_computation | custom fusion | bytes 66048 | tf_op jit(solution)/shard_map/jit(_take)/gather | solution.py:52
  57.6 0.2 bitcast_select_fusion
  57.8 0.1 fusion.32
  57.9 1.0 fusion.17
  58.9 1.0 fusion.18
  59.8 1.0 fusion
  60.8 1.0 fusion.1
  61.8 0.2 pad_maximum_fusion
  62.1 2.3 %copy.14 = f32[1,2,128,2048]{2,1,0,3:T(2,128)} copy(f32[1,2,128,2048]{3,2,1,0:T(8,128)S(1)} %pad_maximum_fusion) | data formatting | bytes 4194304 | tf_op jit(solution)/shard_map/stack | solution.py:62
  64.4 6.5 %all-to-all-start.1 = ((f32[1,2,128,2048]{2,1,0,3:T(2,128)}), f32[1,2,128,2048]{2,1,0,3:T(2,128)S(1)}, u32[]{:S(2)}, u32[]{:S(2)}) async-start(f32[1,2,128,2048]{2,1,0,3:T(2,128)} %copy.14), calls=%async_computation.1 | async-start | bytes 4194304 | tf_op jit(solution)/shard_map/all_to_all | solution.py:80
  70.9 1.9 %cosine_multiply_fusion.1 = (f32[128,1,512]{2,0,1:T(8,128)S(1)}, f32[128,1,512]{2,0,1:T(8,128)}) fusion(s32[512]{0:T(512)S(1)} %iota_add_fusion, s32[128]{0:T(128)S(1)} %iota_add_fusion.1), kind=kLoop, calls=%fused_computation.42 | loop fusion | flops 1114112 | bytes 526848 | tf_op jit(solution)/shard_map/mul | solution.py:35
  72.8 53.6 %all-to-all-done.1 = f32[1,2,128,2048]{2,1,0,3:T(2,128)S(1)} async-done(((f32[1,2,128,2048]{2,1,0,3:T(2,128)}), f32[1,2,128,2048]{2,1,0,3:T(2,128)S(1)}, u32[]{:S(2)}, u32[]{:S(2)}) %all-to-all-start.1) | async-done | bytes 2097184 | tf_op jit(solution)/shard_map/all_to_all | solution.py:80
  126.3 2.4 %copy.16 = f32[1,2,128,128,16]{3,2,1,4,0:T(8,128)} copy(f32[1,2,128,128,16]{2,1,4,3,0:T(2,128)S(1)} %bitcast.59) | data formatting | bytes 4194304 | tf_op jit(solution)/shard_map/all_to_all | solution.py:80
  128.7 5.1 %convolution_bitcast_fusion = f32[128,16,512]{2,0,1:T(8,128)S(1)} fusion(f32[1,2,128,128,16]{3,2,1,4,0:T(8,128)} %copy.16, f32[128,1,512]{2,0,1:T(8,128)} %get-tuple-element.14, f32[128,1,512]{2,0,1:T(8,128)S(1)} %get-tuple-element.13), kind=kOutput, calls=%fused_computation.5 | convolution fusion | flops 3221356544 | bytes 6815744 | tf_op jit(solution)/shard_map/fqnc,fql->ncl/dot_general | solution.py:78
  133.8 4.4 %copy.17 = f32[128,16,512]{2,1,0:T(8,128)} copy(f32[128,16,512]{2,0,1:T(8,128)S(1)} %convolution_bitcast_fusion) | data formatting | bytes 8388608 | tf_op jit(solution)/shard_map/fqnc,fql->ncl/dot_general | solution.py:78
  (8 shorter events, 0.1 us)
Async XLA Ops:
  0.0 2.2 %copy-start = (f32[16,16,1024]{2,1,0:T(8,128)S(1)}, f32[16,16,1024]{2,1,0:T(8,128)}, u32[]{:S(2)}) copy-start(f32[16,16,1024]{2,1,0:T(8,128)} %param.2) | copy-start | bytes 3145732
  3.7 19.7 %copy-start.1 = (s32[256]{0:T(256)S(1)}, s32[256]{0:T(256)}, u32[]{:S(2)}) copy-start(s32[256]{0:T(256)} %param.3) | copy-start | bytes 3076
  7.0 33.0 %all-to-all-start = ((f32[128,1,512]{2,1,0:T(1,128)}), f32[128,1,512]{2,1,0:T(1,128)S(1)}, u32[]{:S(2)}, u32[]{:S(2)}) async-start(f32[128,1,512]{2,1,0:T(1,128)} %reshape.356), calls=%async_computation | async-start | bytes 524288 | tf_op jit(solution)/shard_map/all_to_all | solution.py:70
  45.4 7.5 %collective-permute-start = (f32[1,2,2048,16]{2,3,1,0:T(8,128)S(1)}, f32[1,2,2048,16]{2,3,1,0:T(8,128)S(1)}, u32[]{:S(2)}, u32[]{:S(2)}) collective-permute-start(f32[1,2,2048,16]{2,3,1,0:T(8,128)S(1)} %all_to_all.29), channel_id=1, source_target_pairs={{0,128},{128,0},{1,129},{129,1},{2,130},{130,2},{3,131},{131,3},{4... | collective-permute-start | bytes 786440 | tf_op jit(solution)/shard_map/ppermute | solution.py:17
  64.4 61.9 %all-to-all-start.1 = ((f32[1,2,128,2048]{2,1,0,3:T(2,128)}), f32[1,2,128,2048]{2,1,0,3:T(2,128)S(1)}, u32[]{:S(2)}, u32[]{:S(2)}) async-start(f32[1,2,128,2048]{2,1,0,3:T(2,128)} %copy.14), calls=%async_computation.1 | async-start | bytes 4194304 | tf_op jit(solution)/shard_map/all_to_all | solution.py:80
where the time goes:
time: 139 us; the launch traced here: 138 us
  waiting for transfers between devices  77.1 us (55%)
  starting transfers between devices  23.3 us (17%)
  local copies, waits for them, and re-layouts  21.4 us (15%)
  matrix products  10 us (7%)
  other arithmetic  6.27 us (5%)
    all_to_all x1, waiting for transfers between devices, body(): lax.all_to_all(cross, 'shard', split_axis=3, concat_axis=0, tiled=True)  53.6 us
    all_to_all x1, waiting for transfers between devices, body(): lax.all_to_all(whitened, 'shard', split_axis=0, concat_axis=2, tiled=True)  16.5 us
    all_to_all x1, starting transfers between devices, body(): lax.all_to_all(whitened, 'shard', split_axis=0, concat_axis=2, tiled=True)  16.4 us
    ppermute x1, waiting for transfers between devices, partner_2(): lax.ppermute(x, axis, [(i, i ^ 1 << bit) for i in range(lax.axis_size(axi...  7.05 us
    all_to_all x1, starting transfers between devices, body(): lax.all_to_all(cross, 'shard', split_axis=3, concat_axis=0, tiled=True)  6.46 us
    dot_general x1, matrix products, body(): jnp.einsum('fqnc,fql->ncl', lax.all_to_all(cross, 'shard', split_axis=3,...  5.1 us
    dot_general x1, local copies, waits for them, and re-layouts, body(): jnp.einsum('fqnc,fql->ncl', lax.all_to_all(cross, 'shard', split_axis=3,...  4.44 us
    all_to_all x4, local copies, waits for them, and re-layouts, body(): lax.all_to_all(whitened, 'shard', split_axis=0, concat_axis=2, tiled=True)  3.46 us
  transfers between devices with their start and end apart: 3, of which 3 were waited for; matrix products, arithmetic and copies ran while one was open for 1% of the time, Pallas kernels for 0%

commit v1 on v0

v1 whole, which is shorter than its diff:
```python
import functools

import jax
import jax.numpy as jnp
import numpy as np
from jax import lax
from jax.experimental import pallas as pl
from jax.experimental.pallas import tpu as pltpu
from jax.sharding import PartitionSpec as P

F = 128
L = 1024
LAGS = 512
SEG = 32
water_level = 0.2
epsilon = 1e-05

NX, NZ = 4, 8
NJ = 64
ANY = pl.BlockSpec(memory_space=pl.ANY)
VMEM = pl.BlockSpec(memory_space=pltpu.VMEM)
SMEM = pl.BlockSpec(memory_space=pltpu.SMEM)
MESH = pl.DeviceIdType.MESH
BF = jnp.bfloat16
F32 = jnp.float32


def split_np(table):
    hi = table.astype(np.float32).astype(jnp.bfloat16)
    lo = (table - hi.astype(np.float64)).astype(np.float32).astype(jnp.bfloat16)
    return hi, lo


def forward_table():
    bins = np.arange(F) + 1
    times = np.arange(L)
    angle = 2.0 * np.pi * (bins[:, None] * times[None, :] % L) / L
    taper = 0.5 - 0.5 * np.cos(2.0 * np.pi * times / L)
    return np.concatenate((np.cos(angle) * taper, -np.sin(angle) * taper), axis=0)


def inverse_table():
    bins = np.arange(F) + 1
    shifts = np.arange(LAGS) - LAGS // 2
    angle = 2.0 * np.pi * (bins[:, None] * shifts[None, :] % L) / L
    return np.concatenate((np.cos(angle), -np.sin(angle)), axis=0) / np.sqrt(SEG * F)


def split(v):
    hi = v.astype(BF)
    return hi, (v - hi.astype(F32)).astype(BF)


def dot(a, b, ca, cb):
    return lax.dot_general(a, b, (((ca,), (cb,)), ((), ())), preferred_element_type=F32)


def whiten_kernel(rec_ref, hi_ref, lo_ref, out_ref):
    rec_hi, rec_lo = split(rec_ref[...])
    spec = dot(hi_ref[...], rec_hi, 1, 1) + dot(hi_ref[...], rec_lo, 1, 1) + dot(lo_ref[...], rec_hi, 1, 1)
    re, im = spec[:F], spec[F:]
    mag = jnp.sqrt(re * re + im * im)
    zeros = jnp.zeros((2, mag.shape[1]), F32)
    pad = jnp.concatenate((zeros, mag, zeros), axis=0)
    smooth = pad[0:F]
    for off in range(1, 5):
        smooth = smooth + pad[off : off + F]
    mean = jnp.sum(mag, axis=0, keepdims=True) * (1.0 / F)
    divisor = smooth / 5.0 + water_level * mean + epsilon
    for q, part in enumerate((re, im)):
        white = part / divisor
        for s_hi in range(2):
            out_ref[pl.ds(2 * q + s_hi, F, stride=4), :] = white[:, 128 * s_hi : 128 * (s_hi + 1)]


def events():
    out = []
    for dz in (0, 1, -1, 2, -2, 3, -3, 4):
        for dx in (0, 1, -1, 2):
            if (dz, dx) == (0, 0):
                continue
            az, ax = abs(dz), abs(dx)
            out.append((1.0 * ax + 2.0 * az * (1.0 if ax == 0 else 1.2) + 0.3 * ax, 0, dz, dx))
            out.append((1.0 * az + 2.0 * ax + (0.5 if ax else 0), 1, dz, dx))
    out.sort(key=lambda e: e[0])
    return [e[1:] for e in out]


def comm_kernel(idx_ref, w_ref, g_ref, wo_ref, a_ref, gm_ref, pick_ref, y_ref,
                a_send, a_recv, y_send, y_recv, wo_send, wo_recv, g_send, g_recv, sib_recv):
    h = lax.axis_index("half")
    s = lax.axis_index("shard")
    yh, j = s // NJ, s % NJ
    z, x, k = j // 8, (j // 2) % 4, j % 2

    barrier = pltpu.get_barrier_semaphore()

    def greet(i, carry):
        pl.semaphore_signal(barrier, inc=1, device_id=(h, yh * NJ + (j + i) % NJ), device_id_type=MESH)
        return carry

    lax.fori_loop(1, NJ, greet, 0)
    ring_y = [(h, (1 - yh) * NJ + j), (1 - h, yh * NJ + j), (1 - h, (1 - yh) * NJ + j)]
    for dev in ring_y:
        pl.semaphore_signal(barrier, inc=1, device_id=dev, device_id_type=MESH)
    pl.semaphore_wait(barrier, NJ + 2)

    def remote(src, dst, ssem, rsem, dev):
        return pltpu.make_async_remote_copy(
            src_ref=src, dst_ref=dst, send_sem=ssem, recv_sem=rsem, device_id=dev, device_id_type=MESH
        )

    def scatter(i, carry):
        t = (j + i) % NJ
        remote(w_ref.at[t], a_ref.at[j], a_send, a_recv, (h, yh * NJ + t)).start()
        return carry

    lax.fori_loop(1, NJ, scatter, 0)
    wo = remote(w_ref, wo_ref, wo_send, wo_recv, ring_y[1])
    wo.start()
    a_ref[j] = w_ref[j]
    all_a = remote(w_ref.at[pl.ds(0, NJ - 1)], a_ref.at[pl.ds(0, NJ - 1)], a_send, a_recv, ring_y[0])
    all_a.wait_send()
    all_a.wait_recv()

    lane_c = lax.broadcasted_iota(jnp.int32, (8, 128), 1) & 15

    def pick(n, carry):
        q = idx_ref[n]
        p = q >> 4
        c = jnp.where((p >> 6) == yh, q & 15, 99)
        v = jnp.where(lane_c == c, a_ref[p & (NJ - 1)], 0.0)
        gm_ref[pl.ds(n, 8, stride=256), :] = v
        return carry

    lax.fori_loop(0, 256, pick, 0, unroll=8)
    row = lax.broadcasted_iota(jnp.int32, (8, 128), 0)
    col = lax.broadcasted_iota(jnp.int32, (8, 128), 1)
    fold = jnp.where((col >> 4) == row, 1.0, 0.0).astype(BF)
    for e in range(8):
        v = gm_ref[256 * e : 256 * (e + 1), :]
        hi = v.astype(BF)
        rest = v - hi.astype(F32)
        mid = rest.astype(BF)
        lo = (rest - mid.astype(F32)).astype(BF)
        got = dot(fold, hi, 1, 1) + dot(fold, mid, 1, 1) + dot(fold, lo, 1, 1)
        pick_ref[0, 8 * e : 8 * (e + 1), :] = got[:, :128]
        pick_ref[1, 8 * e : 8 * (e + 1), :] = got[:, 128:]

    trades = [
        remote(pick_ref.at[h], y_ref.at[0], y_send.at[0], y_recv.at[0], ring_y[0]),
        remote(pick_ref.at[1 - h], y_ref.at[1], y_send.at[1], y_recv.at[1], ring_y[1]),
        remote(pick_ref.at[1 - h], y_ref.at[2], y_send.at[2], y_recv.at[2], ring_y[2]),
    ]
    for t in trades:
        t.start()
    for t in trades:
        t.wait()
    own = pick_ref[h] + y_ref[0]
    other = y_ref[1] + y_ref[2]
    for f2 in range(2):
        g_ref[j, f2, 0] = own[32 * f2 : 32 * f2 + 32]
        g_ref[j, f2, 1] = other[32 * f2 : 32 * f2 + 32]

    def place(dz, dx):
        return ((z + dz + NZ) % NZ) * 8 + ((x + dx + NX) % NX) * 2 + k

    def send(b, f2, dz, dx):
        blk = g_ref.at[b, f2]
        remote(blk, blk, g_send, g_recv.at[b, f2], (h, yh * NJ + place(dz, dx))).start()

    def share(b, f2):
        blk = g_ref.at[b, f2]
        remote(blk, blk, g_send, sib_recv, (h, s + 1 - 2 * k)).start()

    for dx in (1, -1, 2):
        send(j, 0, 0, dx)
    for dz in (1, -1):
        send(j, 0, dz, 0)
    for dx in (1, -1):
        send(j, 1, 0, dx)
    for dz in (1, -1, 2, -2, 3, -3, 4):
        send(j, 1, dz, 0)
    share(j, 0)
    share(j, 1)
    for f2, dz, dx in events():
        b = place(dz, dx)
        blk = g_ref.at[b, f2]
        remote(blk, blk, g_send, g_recv.at[b, f2], ring_y[0]).wait_recv()
        if f2 == 0:
            xs = (x + dx + NX) % NX
            if dz == 0:
                send(b, 0, 1, 0)
                send(b, 0, -1, 0)
            elif dz in (-1, -2):
                send(b, 0, 1, 0)
            elif dz in (1, 2):
                send(b, 0, -1, 0)
            elif dz == -3:
                @pl.when(xs % 2 == 0)
                def _():
                    send(b, 0, 1, 0)
            elif dz == 3:
                @pl.when(xs % 2 == 1)
                def _():
                    send(b, 0, -1, 0)
        else:
            zs = (z + dz + NZ) % NZ
            if dx == 0:
                send(b, 1, 0, 1)
                send(b, 1, 0, -1)
            elif dx == -1:
                @pl.when(zs % 2 == 0)
                def _():
                    send(b, 1, 0, 1)
            elif dx == 1:
                @pl.when(zs % 2 == 1)
                def _():
                    send(b, 1, 0, -1)
        share(b, f2)
    half_g = g_ref.at[pl.ds(0, NJ // 2)]
    remote(half_g, half_g, g_send, sib_recv, ring_y[0]).wait_recv()
    most_g = g_ref.at[pl.ds(0, NJ - 1)]
    remote(most_g, most_g, g_send, sib_recv, ring_y[0]).wait_send()
    wo.wait()


def output_kernel(g_ref, w_ref, wo_ref, hi_ref, lo_ref, out_ref, lhs_ref, x_ref, xt_ref, stage_ref, sem):
    lane = lax.broadcasted_iota(jnp.int32, (16, 128), 1)
    parts = []
    for ref in (w_ref, wo_ref):
        for e in range(4):
            parts.append(ref[pl.ds(e, F, stride=4), :].T)
    v = [parts[i // 8][16 * (i % 8) : 16 * (i % 8) + 16, :] for i in range(64)]
    for bit in range(6):
        step = 1 << bit
        low = (lane & step) == 0
        for i in range(64):
            if i & step:
                continue
            a, b = v[i], v[i + step]
            v[i] = jnp.where(low, a, pltpu.roll(b, step, 1))
            v[i + step] = jnp.where(low, pltpu.roll(a, 128 - step, 1), b)
    first = (lane & 16) == 0
    top = lane < 64
    for g in range(64):
        a = v[g]
        b = jnp.where(first, pltpu.roll(a, 112, 1), -pltpu.roll(a, 16, 1))
        rows = []
        for r in (a, b):
            rows.append(jnp.where(top, r, 0.0))
            rows.append(jnp.where(top, 0.0, r))
        m = jnp.concatenate(rows, axis=0)
        hi, lo = split(m)
        lhs_ref[g] = jnp.concatenate((hi, lo), axis=0)

    def cross(g, carry):
        src = jnp.concatenate((g_ref[g], g_ref[g + 64]), axis=0)
        hi, lo = split(src)
        res = dot(lhs_ref[g], jnp.concatenate((hi, lo), axis=1), 1, 0)
        res = res[:64, :128] + (res[:64, 128:] + res[64:, :128])
        for i in range(4):
            x_ref[pl.ds(64 * i + g, 16, stride=256), :] = res[16 * i : 16 * i + 16]
        return carry

    lax.fori_loop(0, 64, cross, 0, unroll=4)
    copies = []
    for half in range(2):
        th = hi_ref[:, 256 * half : 256 * half + 256]
        tl = lo_ref[:, 256 * half : 256 * half + 256]
        for c in range(16):
            if half == 0:
                hi, lo = split(x_ref[256 * c : 256 * c + 256, :].T)
                xt_ref[0, c], xt_ref[1, c] = hi, lo
            hi, lo = xt_ref[0, c], xt_ref[1, c]
            res = dot(hi, th, 1, 0) + dot(hi, tl, 1, 0) + dot(lo, th, 1, 0)
            for b in range(2):
                stage_ref[2 * half + b, pl.ds(c, 128, stride=16), :] = res[:, 128 * b : 128 * b + 128]
        for b in range(2 * half, 2 * half + 2):
            copy = pltpu.make_async_copy(stage_ref.at[b], out_ref.at[:, pl.ds(128 * b, 128)], sem.at[b])
            copy.start()
            copies.append(copy)
    for copy in copies:
        copy.wait()


def body(recording, source_channels):
    fwd_hi, fwd_lo = (jnp.asarray(t) for t in split_np(forward_table()))
    inv_hi, inv_lo = (jnp.asarray(t) for t in split_np(inverse_table()))
    rec = recording.reshape(256, L)
    w = pl.pallas_call(
        whiten_kernel,
        out_shape=jax.ShapeDtypeStruct((512, 128), F32),
        in_specs=[VMEM] * 3,
        out_specs=VMEM,
        name="whiten",
    )(rec, fwd_hi, fwd_lo)
    dma = pltpu.SemaphoreType.DMA
    g, wo = pl.pallas_call(
        comm_kernel,
        out_shape=(
            jax.ShapeDtypeStruct((NJ, 2, 2, 32, 128), F32),
            jax.ShapeDtypeStruct((NJ, 8, 128), F32),
        ),
        in_specs=[SMEM, VMEM],
        out_specs=(VMEM, VMEM),
        scratch_shapes=[
            pltpu.VMEM((NJ, 8, 128), F32),
            pltpu.VMEM((2048, 128), F32),
            pltpu.VMEM((2, 64, 128), F32),
            pltpu.VMEM((3, 64, 128), F32),
            dma, dma, dma((3,)), dma((3,)), dma, dma, dma, dma((NJ, 2)), dma,
        ],
        compiler_params=pltpu.CompilerParams(collective_id=0, has_side_effects=True),
        name="exchange",
    )(source_channels, w.reshape(NJ, 8, 128))
    out = pl.pallas_call(
        output_kernel,
        out_shape=jax.ShapeDtypeStruct((128 * 16, LAGS), F32),
        in_specs=[VMEM] * 5,
        out_specs=ANY,
        scratch_shapes=[
            pltpu.VMEM((64, 128, 128), BF),
            pltpu.VMEM((16 * 256, 128), F32),
            pltpu.VMEM((2, 16, 128, 256), BF),
            pltpu.VMEM((4, 2048, 128), F32),
            dma((4,)),
        ],
        name="correlate",
    )(g.reshape(F, 64, 128), w, wo.reshape(512, 128), inv_hi, inv_lo)
    return out.reshape(128, 16, LAGS)


def solution(mesh):
    return jax.shard_map(
        body,
        mesh=mesh,
        in_specs=(P("half", "shard", None), P()),
        out_specs=P("half", "shard", None),
        check_vma=False,
    )
```

time: 139 us -> 70.9 us (0.51)
  waiting for transfers between devices: 77.1 us -> 0 us
  Pallas kernels: 0 us -> 70.7 us
  starting transfers between devices: 23.3 us -> 0 us
  local copies, waits for them, and re-layouts: 21.4 us -> 0 us
  matrix products: 10 us -> 0 us
  other arithmetic: 6.27 us -> 0 us
    pallas_call x0 -> x3, Pallas kernels: none -> 70.7 us  [the longest x1 55.5 us: body(): pl.pallas_call(comm_kernel, out_shape=(jax.ShapeDtypeStruct((NJ, 2, 2, 32...]
    all_to_all x2 -> x0, waiting for transfers between devices: 70 us -> none  [the longest x1 53.6 us: body(): lax.all_to_all(cross, 'shard', split_axis=3, concat_axis=0, tiled=True)]
    all_to_all x2 -> x0, starting transfers between devices: 22.9 us -> none  [the longest x1 16.4 us: body(): lax.all_to_all(whitened, 'shard', split_axis=0, concat_axis=2, tiled=True)]
    dot_general x6 -> x0, matrix products: 10 us -> none  [the longest x1 5.1 us: body(): jnp.einsum('fqnc,fql->ncl', lax.all_to_all(cross, 'shard', split_axis=3,...]
    ppermute x1 -> x0, waiting for transfers between devices: 7.05 us -> none  [partner_2(): lax.ppermute(x, axis, [(i, i ^ 1 << bit) for i in range(lax.axis_size(axi...]
    all_to_all x5 -> x0, local copies, waits for them, and re-layouts: 5.87 us -> none  [the longest x4 3.46 us: body(): lax.all_to_all(whitened, 'shard', split_axis=0, concat_axis=2, tiled=True)]
    dot_general x1 -> x0, local copies, waits for them, and re-layouts: 4.44 us -> none  [body(): jnp.einsum('fqnc,fql->ncl', lax.all_to_all(cross, 'shard', split_axis=3,...]
    mul x3 -> x0, other arithmetic: 4.06 us -> none  [the longest x1 2.16 us: forward_table(): jnp.cos(angle) * taper[None, :]]
  transfers between devices with their start and end apart: 3 -> 0, of which waited for: 3 -> 0; matrix products, arithmetic and copies ran while one was open for 1% -> 0% of each run, Pallas kernels for 0% -> 0%
where the time goes in v1:
time: 70.9 us; the launch traced here: 70.7 us
  Pallas kernels  70.7 us (100%)
    pallas_call x1, Pallas kernels, body(): pl.pallas_call(comm_kernel, out_shape=(jax.ShapeDtypeStruct((NJ, 2, 2, 32...  55.5 us
    pallas_call x1, Pallas kernels, body(): pl.pallas_call(output_kernel, out_shape=jax.ShapeDtypeStruct((128 * 16, L...  12.3 us
    pallas_call x1, Pallas kernels, body(): pl.pallas_call(whiten_kernel, out_shape=jax.ShapeDtypeStruct((512, 128),...  2.97 us

profile of v1, /device:TPU:1, one launch (start us, length us, event | category | flops | bytes accessed | tf_op | source)
XLA Modules:
  0.0 70.7 jit_solution(16062984439065138138)
XLA Ops:
  0.0 3.0 %whiten.1.w_ref = f32[512,128]{1,0:T(8,128)} custom-call(f32[256,1024]{1,0:T(8,128)} %bitcast.7, bf16[256,1024]{1,0:T(8,128)(2,1)} %constant.8.clone.hi_ref, bf16[256,1024]{1,0:T(8,128)(2,1)} %constant.9.clone.lo_ref), custom_call_target="tpu_custom_call" | custom-call | tf_op jit(solution)/shard_map/whiten/pallas_call | solution.py:291
  3.0 55.5 %exchange.1 = (f32[64,2,2,32,128]{4,3,2,1,0:T(8,128)}, f32[64,8,128]{2,1,0:T(8,128)}) custom-call(s32[256]{0:T(256)} %idx_ref.1, f32[64,8,128]{2,1,0:T(8,128)} %bitcast.6), custom_call_target="tpu_custom_call" | custom-call | tf_op jit(solution)/shard_map/exchange/pallas_call | solution.py:299
  58.4 12.3 %correlate.1 = f32[2048,512]{1,0:T(8,128)} custom-call(f32[128,64,128]{2,1,0:T(8,128)} %bitcast.5, f32[512,128]{1,0:T(8,128)} %whiten.1.w_ref, f32[512,128]{1,0:T(8,128)} %bitcast.8, bf16[256,512]{1,0:T(8,128)(2,1)} %constant.10.clone.hi_ref, bf16[256,512]{1,0:T(8,128)(2,1)} %constant.11.clone.lo_ref), custom_call_target="tpu_custom_call" | custom-call | tf_op jit(solution)/shard_map/correlate/pallas_call | solution.py:317

commit v2 on v1

v2 whole, which is shorter than its diff:
```python
import functools

import jax
import jax.numpy as jnp
import numpy as np
from jax import lax
from jax.experimental import pallas as pl
from jax.experimental.pallas import tpu as pltpu
from jax.sharding import PartitionSpec as P

F = 128
L = 1024
LAGS = 512
SEG = 32
water_level = 0.2
epsilon = 1e-05

NX, NZ = 4, 8
NJ = 64
ANY = pl.BlockSpec(memory_space=pl.ANY)
VMEM = pl.BlockSpec(memory_space=pltpu.VMEM)
SMEM = pl.BlockSpec(memory_space=pltpu.SMEM)
MESH = pl.DeviceIdType.MESH
BF = jnp.bfloat16
F32 = jnp.float32


def split_np(table):
    hi = table.astype(np.float32).astype(jnp.bfloat16)
    lo = (table - hi.astype(np.float64)).astype(np.float32).astype(jnp.bfloat16)
    return hi, lo


def forward_table():
    bins = np.arange(F) + 1
    times = np.arange(L)
    angle = 2.0 * np.pi * (bins[:, None] * times[None, :] % L) / L
    taper = 0.5 - 0.5 * np.cos(2.0 * np.pi * times / L)
    return np.concatenate((np.cos(angle) * taper, -np.sin(angle) * taper), axis=0)


def inverse_table():
    bins = np.arange(F) + 1
    shifts = np.arange(LAGS) - LAGS // 2
    angle = 2.0 * np.pi * (bins[:, None] * shifts[None, :] % L) / L
    return np.concatenate((np.cos(angle), -np.sin(angle)), axis=0) / np.sqrt(SEG * F)


def split(v):
    hi = v.astype(BF)
    return hi, (v - hi.astype(F32)).astype(BF)


def dot(a, b, ca, cb):
    return lax.dot_general(a, b, (((ca,), (cb,)), ((), ())), preferred_element_type=F32)


OFF_Z = (1, -1, 2, -2, 3, -3, 4)


def events():
    out = []
    for dz in (0,) + OFF_Z:
        for dx in (0, 1, -1, 2):
            if (dz, dx) == (0, 0):
                continue
            az, ax = abs(dz), abs(dx)
            out.append((1.0 * ax + 2.0 * az * (1.0 if ax == 0 else 1.2) + 0.3 * ax, 0, dz, dx))
            out.append((1.0 * az + 2.0 * ax + (0.5 if ax else 0), 1, dz, dx))
    out.sort(key=lambda e: e[0])
    return [e[1:] for e in out]


def whiten(rec_ref, hi_ref, lo_ref, out_ref):
    rec_hi, rec_lo = split(rec_ref[...])
    spec = dot(hi_ref[...], rec_hi, 1, 1) + dot(hi_ref[...], rec_lo, 1, 1) + dot(lo_ref[...], rec_hi, 1, 1)
    re, im = spec[:F], spec[F:]
    mag = jnp.sqrt(re * re + im * im)
    zeros = jnp.zeros((2, mag.shape[1]), F32)
    pad = jnp.concatenate((zeros, mag, zeros), axis=0)
    smooth = pad[0:F]
    for off in range(1, 5):
        smooth = smooth + pad[off : off + F]
    mean = jnp.sum(mag, axis=0, keepdims=True) * (1.0 / F)
    divisor = smooth / 5.0 + water_level * mean + epsilon
    for q, part in enumerate((re, im)):
        white = part / divisor
        for s_hi in range(2):
            out_ref[pl.ds(2 * q + s_hi, F, stride=4), :] = white[:, 128 * s_hi : 128 * (s_hi + 1)]


def swap(v, bit, lane):
    step = 1 << bit
    low = (lane & step) == 0
    v = list(v)
    for i in range(len(v)):
        if i & step:
            continue
        a, b = v[i], v[i + step]
        v[i] = jnp.where(low, a, pltpu.roll(b, step, 1))
        v[i + step] = jnp.where(low, pltpu.roll(a, 128 - step, 1), b)
    return v


def lanes():
    return lax.broadcasted_iota(jnp.int32, (16, 128), 1)


def receivers_first(ref, mid_ref, side):
    v = []
    for e in range(4):
        t = ref[pl.ds(e, F, stride=4), :].T
        v += [t[16 * i : 16 * i + 16] for i in range(8)]
    for bit in range(5):
        v = swap(v, bit, lanes())
    for i in range(32):
        mid_ref[side, i] = v[i]


def receivers_last(mid_ref, lhs_ref):
    lane = lanes()
    first = (lane & 16) == 0
    top = lane < 64
    low = (lane & 32) == 0
    for i in range(32):
        a, b = mid_ref[0, i], mid_ref[1, i]
        pair = (jnp.where(low, a, pltpu.roll(b, 32, 1)), jnp.where(low, pltpu.roll(a, 96, 1), b))
        for half in range(2):
            a = pair[half]
            b = jnp.where(first, pltpu.roll(a, 112, 1), -pltpu.roll(a, 16, 1))
            rows = []
            for r in (a, b):
                rows.append(jnp.where(top, r, 0.0))
                rows.append(jnp.where(top, 0.0, r))
            hi, lo = split(jnp.concatenate(rows, axis=0))
            lhs_ref[32 * half + i] = jnp.concatenate((hi, lo), axis=0)


def exchange_kernel(idx_ref, rec_hbm, hi_hbm, lo_hbm, x_ref, rec_ref, hi_ref, lo_ref, w_ref, wo_ref, z_ref, a_ref,
                    gm_ref, pick_ref, y_ref, g_ref, mid_ref, lhs_ref,
                    load, z_send, z_recv, a_send, a_recv, y_send, y_recv, wo_send, wo_recv, g_send, g_recv):
    h = lax.axis_index("half")
    s = lax.axis_index("shard")
    yh, u, k = s // NJ, (s % NJ) // 2, s % 2
    z, x = u // NX, u % NX
    j = k * 32 + u

    def device(zz, xx, kk):
        return (h, yh * NJ + (zz * NX + xx) * 2 + kk)

    def zat(d):
        return (z + d + NZ) % NZ

    def xat(d):
        return (x + d + NX) % NX

    def remote(src, dst, ssem, rsem, dev):
        return pltpu.make_async_remote_copy(
            src_ref=src, dst_ref=dst, send_sem=ssem, recv_sem=rsem, device_id=dev, device_id_type=MESH
        )

    plane = [(xat(d), kk) for d in (0, 1, -1, 2) for kk in (k, 1 - k)][1:]
    ring_y = [(h, (1 - yh) * NJ + s % NJ), (1 - h, s), (1 - h, (1 - yh) * NJ + s % NJ)]
    barrier = pltpu.get_barrier_semaphore()
    for dev in [device(zat(d), x, k) for d in OFF_Z] + [device(z, *p) for p in plane] + ring_y:
        pl.semaphore_signal(barrier, inc=1, device_id=dev, device_id_type=MESH)
    loads = [
        pltpu.make_async_copy(a, b, load.at[i])
        for i, (a, b) in enumerate(((rec_hbm, rec_ref), (hi_hbm, hi_ref), (lo_hbm, lo_ref)))
    ]
    for c in loads:
        c.start()
    for c in loads:
        c.wait()
    whiten(rec_ref, hi_ref, lo_ref, w_ref)
    pl.semaphore_wait(barrier, 17)

    def rows(kk, zz, n):
        return pl.ds(pl.multiple_of((kk * 32 + zz * NX) * 8, 8), n)

    for d in OFF_Z:
        for kk in range(2):
            remote(
                w_ref.at[rows(kk, zat(d), 32)], z_ref.at[kk, z], z_send, z_recv.at[kk, z], device(zat(d), x, k)
            ).start()
    wo = remote(w_ref, wo_ref, wo_send, wo_recv, ring_y[1])
    wo.start()
    for kk in range(2):
        z_ref[kk, z] = w_ref[rows(kk, z, 32), :]
    receivers_first(w_ref, mid_ref, 0)
    for d in (0,) + OFF_Z:
        zs = zat(d)
        if d:
            for kk in range(2):
                remote(z_ref.at[kk, zs], z_ref.at[kk, zs], z_send, z_recv.at[kk, zs], ring_y[0]).wait_recv()
        mine = k * 32 + zs * NX + x
        for xx, kk in plane:
            src = z_ref.at[kk, zs, pl.ds(pl.multiple_of(xx * 8, 8), 8)]
            remote(src, a_ref.at[mine], a_send, a_recv, device(z, xx, kk)).start()
        a_ref[mine] = z_ref[k, zs, pl.ds(pl.multiple_of(x * 8, 8), 8), :]
    some_a = remote(a_ref.at[pl.ds(0, 56)], a_ref.at[pl.ds(0, 56)], a_send, a_recv, ring_y[0])
    some_a.wait_recv()

    lane_c = lax.broadcasted_iota(jnp.int32, (8, 128), 1) & 15

    def pick(n, carry):
        q = idx_ref[n]
        p = q >> 4
        c = jnp.where((p >> 6) == yh, q & 15, 99)
        v = jnp.where(lane_c == c, a_ref[(p & 1) * 32 + ((p & 63) >> 1)], 0.0)
        gm_ref[pl.ds(n, 8, stride=256), :] = v
        return carry

    lax.fori_loop(0, 256, pick, 0, unroll=8)
    row = lax.broadcasted_iota(jnp.int32, (8, 128), 0)
    col = lax.broadcasted_iota(jnp.int32, (8, 128), 1)
    fold = jnp.where((col >> 4) == row, 1.0, 0.0).astype(BF)
    for e in range(8):
        v = gm_ref[256 * e : 256 * (e + 1), :]
        hi = v.astype(BF)
        rest = v - hi.astype(F32)
        mid = rest.astype(BF)
        lo = (rest - mid.astype(F32)).astype(BF)
        got = dot(fold, hi, 1, 1) + dot(fold, mid, 1, 1) + dot(fold, lo, 1, 1)
        pick_ref[0, 8 * e : 8 * (e + 1), :] = got[:, :128]
        pick_ref[1, 8 * e : 8 * (e + 1), :] = got[:, 128:]

    trades = [
        remote(pick_ref.at[h], y_ref.at[0], y_send.at[0], y_recv.at[0], ring_y[0]),
        remote(pick_ref.at[1 - h], y_ref.at[1], y_send.at[1], y_recv.at[1], ring_y[1]),
        remote(pick_ref.at[1 - h], y_ref.at[2], y_send.at[2], y_recv.at[2], ring_y[2]),
    ]
    for t in trades:
        t.start()
    wo.wait()
    receivers_first(wo_ref, mid_ref, 1)
    receivers_last(mid_ref, lhs_ref)
    for t in trades:
        t.wait()
    own = pick_ref[h] + y_ref[0]
    other = y_ref[1] + y_ref[2]
    for f2 in range(2):
        g_ref[j, f2, 0] = own[32 * f2 : 32 * f2 + 32]
        g_ref[j, f2, 1] = other[32 * f2 : 32 * f2 + 32]

    def send(u2, f2, dz, dx):
        blk = g_ref.at[k * 32 + u2, f2]
        remote(blk, blk, g_send, g_recv.at[k * 32 + u2, f2], device(zat(dz), xat(dx), k)).start()

    def share(u2, f2):
        blk = g_ref.at[k * 32 + u2, f2]
        remote(blk, blk, g_send, g_recv.at[k * 32 + u2, f2], device(z, x, 1 - k)).start()

    def arrived(kk, u2, f2):
        blk = g_ref.at[kk * 32 + u2, f2]
        remote(blk, blk, g_send, g_recv.at[kk * 32 + u2, f2], ring_y[0]).wait_recv()

    def cross(u2, f2):
        arrived(1 - k, u2, f2)
        g = u2 * 2 + f2
        src = jnp.concatenate((g_ref[u2, f2].reshape(64, 128), g_ref[32 + u2, f2].reshape(64, 128)), axis=0)
        hi, lo = split(src)
        res = dot(lhs_ref[g], jnp.concatenate((hi, lo), axis=1), 1, 0)
        res = res[:64, :128] + (res[:64, 128:] + res[64:, :128])
        for i in range(4):
            x_ref[pl.ds(64 * i + g, 16, stride=256), :] = res[16 * i : 16 * i + 16]

    for dx in (1, -1, 2):
        send(u, 0, 0, dx)
    for dz in (1, -1):
        send(u, 0, dz, 0)
    for dx in (1, -1):
        send(u, 1, 0, dx)
    for dz in OFF_Z:
        send(u, 1, dz, 0)
    share(u, 0)
    share(u, 1)
    todo = [(u, 0), (u, 1)]
    for f2, dz, dx in events():
        zs, xs = zat(dz), xat(dx)
        b = zs * NX + xs
        arrived(k, b, f2)
        if f2 == 0:
            if dz == 0:
                send(b, 0, 1, 0)
                send(b, 0, -1, 0)
            elif dz in (-1, -2):
                send(b, 0, 1, 0)
            elif dz in (1, 2):
                send(b, 0, -1, 0)
            elif dz == -3:
                @pl.when(xs % 2 == 0)
                def _():
                    send(b, 0, 1, 0)
            elif dz == 3:
                @pl.when(xs % 2 == 1)
                def _():
                    send(b, 0, -1, 0)
        else:
            if dx == 0:
                send(b, 1, 0, 1)
                send(b, 1, 0, -1)
            elif dx == -1:
                @pl.when(zs % 2 == 0)
                def _():
                    send(b, 1, 0, 1)
            elif dx == 1:
                @pl.when(zs % 2 == 1)
                def _():
                    send(b, 1, 0, -1)
        share(b, f2)
        todo.append((b, f2))
        if len(todo) > 3:
            cross(*todo.pop(0))
    for t in todo:
        cross(*t)
    most_g = g_ref.at[pl.ds(0, NJ - 1)]
    remote(most_g, most_g, g_send, a_recv, ring_y[0]).wait_send()
    some_a.wait_send()
    sent_z = w_ref.at[pl.ds(0, 448)]
    remote(sent_z, sent_z, z_send, a_recv, ring_y[0]).wait_send()


def output_kernel(x_ref, hi_ref, lo_ref, out_ref, xt_ref, stage_ref, sem):
    copies = []
    for half in range(2):
        th = hi_ref[:, 256 * half : 256 * half + 256]
        tl = lo_ref[:, 256 * half : 256 * half + 256]
        for c in range(16):
            if half == 0:
                hi, lo = split(x_ref[256 * c : 256 * c + 256, :].T)
                xt_ref[0, c], xt_ref[1, c] = hi, lo
            hi, lo = xt_ref[0, c], xt_ref[1, c]
            res = dot(hi, th, 1, 0) + dot(hi, tl, 1, 0) + dot(lo, th, 1, 0)
            for b in range(2):
                stage_ref[2 * half + b, pl.ds(c, 128, stride=16), :] = res[:, 128 * b : 128 * b + 128]
        for b in range(2 * half, 2 * half + 2):
            copy = pltpu.make_async_copy(stage_ref.at[b], out_ref.at[:, pl.ds(128 * b, 128)], sem.at[b])
            copy.start()
            copies.append(copy)
    for copy in copies:
        copy.wait()


def body(recording, source_channels):
    fwd_hi, fwd_lo = (jnp.asarray(t) for t in split_np(forward_table()))
    inv_hi, inv_lo = (jnp.asarray(t) for t in split_np(inverse_table()))
    dma = pltpu.SemaphoreType.DMA
    cross = pl.pallas_call(
        exchange_kernel,
        out_shape=jax.ShapeDtypeStruct((16 * 256, 128), F32),
        in_specs=[SMEM, ANY, ANY, ANY],
        out_specs=VMEM,
        scratch_shapes=[
            pltpu.VMEM((256, L), F32),
            pltpu.VMEM((256, L), BF),
            pltpu.VMEM((256, L), BF),
            pltpu.VMEM((512, 128), F32),
            pltpu.VMEM((512, 128), F32),
            pltpu.VMEM((2, NZ, 32, 128), F32),
            pltpu.VMEM((NJ, 8, 128), F32),
            pltpu.VMEM((2048, 128), F32),
            pltpu.VMEM((2, 64, 128), F32),
            pltpu.VMEM((3, 64, 128), F32),
            pltpu.VMEM((NJ, 2, 2, 32, 128), F32),
            pltpu.VMEM((2, 32, 16, 128), F32),
            pltpu.VMEM((64, 128, 128), BF),
            dma((3,)), dma, dma((2, NZ)), dma, dma, dma((3,)), dma((3,)), dma, dma, dma, dma((NJ, 2)),
        ],
        compiler_params=pltpu.CompilerParams(collective_id=0, has_side_effects=True),
        name="exchange",
    )(source_channels, recording.reshape(256, L), fwd_hi, fwd_lo)
    out = pl.pallas_call(
        output_kernel,
        out_shape=jax.ShapeDtypeStruct((128 * 16, LAGS), F32),
        in_specs=[VMEM] * 3,
        out_specs=ANY,
        scratch_shapes=[
            pltpu.VMEM((2, 16, 128, 256), BF),
            pltpu.VMEM((4, 2048, 128), F32),
            dma((4,)),
        ],
        name="correlate",
    )(cross, inv_hi, inv_lo)
    return out.reshape(128, 16, LAGS)


def solution(mesh):
    return jax.shard_map(
        body,
        mesh=mesh,
        in_specs=(P("half", "shard", None), P()),
        out_specs=P("half", "shard", None),
        check_vma=False,
    )
```

time: 70.9 us -> 67 us (0.945)
  Pallas kernels: 70.7 us -> 66.9 us
    pallas_call x1, Pallas kernels: 12.3 us -> 5.93 us  [body(): pl.pallas_call(output_kernel, out_shape=jax.ShapeDtypeStruct((128 * 16, L...]
    pallas_call x2 -> x1, Pallas kernels: 58.4 us -> 60.9 us  [body(): pl.pallas_call(exchange_kernel, out_shape=jax.ShapeDtypeStruct((16 * 256,...]
where the time goes in v2:
time: 67 us; the launch traced here: 66.9 us
  Pallas kernels  66.9 us (100%)
    pallas_call x1, Pallas kernels, body(): pl.pallas_call(exchange_kernel, out_shape=jax.ShapeDtypeStruct((16 * 256,...  60.9 us
    pallas_call x1, Pallas kernels, body(): pl.pallas_call(output_kernel, out_shape=jax.ShapeDtypeStruct((128 * 16, L...  5.93 us

profile of v2, /device:TPU:1, one launch (start us, length us, event | category | flops | bytes accessed | tf_op | source)
XLA Modules:
  0.0 66.9 jit_solution(11721954800186167981)
XLA Ops:
  0.0 60.9 %exchange.1.x_ref = f32[4096,128]{1,0:T(8,128)} custom-call(s32[256]{0:T(256)} %idx_ref.1, f32[256,1024]{1,0:T(8,128)} %bitcast.2, bf16[256,1024]{1,0:T(8,128)(2,1)} %constant.8.clone.hi_hbm, bf16[256,1024]{1,0:T(8,128)(2,1)} %constant.9.clone.lo_hbm), custom_call_target="tpu_custom_call" | custom-call | tf_op jit(solution)/shard_map/exchange/pallas_call | solution.py:349
  60.9 5.9 %correlate.1 = f32[2048,512]{1,0:T(8,128)} custom-call(f32[4096,128]{1,0:T(8,128)} %exchange.1.x_ref, bf16[256,512]{1,0:T(8,128)(2,1)} %constant.10.clone.hi_ref, bf16[256,512]{1,0:T(8,128)(2,1)} %constant.11.clone.lo_ref), custom_call_target="tpu_custom_call" | custom-call | tf_op jit(solution)/shard_map/correlate/pallas_call | solution.py:373

commit v3 on v2

--- a/solution.py
+++ b/solution.py
@@ -56,19 +56,36 @@
 
 
 OFF_Z = (1, -1, 2, -2, 3, -3, 4)
-
-
-def events():
-    out = []
-    for dz in (0,) + OFF_Z:
-        for dx in (0, 1, -1, 2):
-            if (dz, dx) == (0, 0):
-                continue
-            az, ax = abs(dz), abs(dx)
-            out.append((1.0 * ax + 2.0 * az * (1.0 if ax == 0 else 1.2) + 0.3 * ax, 0, dz, dx))
-            out.append((1.0 * az + 2.0 * ax + (0.5 if ax else 0), 1, dz, dx))
-    out.sort(key=lambda e: e[0])
-    return [e[1:] for e in out]
+FIRST = (
+    ((1, 0), (-1, 0), (0, 1), (0, -1), (0, -2)),
+    ((-1, 0), (2, 0), (1, 0), (0, 1), (0, -1)),
+)
+GATHER = (
+    (0, 0, 0, None), (1, 0, 0, None), (0, 1, 0, ((1, 0), (0, -1), (0, 1))), (0, 0, 1, ()),
+    (1, -1, 0, ((-1, 0), (0, -1))), (0, 0, -1, ()), (0, -1, 0, ((-1, 0), (0, 1), (0, -1))),
+    (1, 0, 1, ((0, 1), (-1, 0))), (0, -1, 0, None), (0, 0, -1, None), (1, 1, 0, ((3, 0), (0, 1))), (1, 1, 0, None),
+    (0, 0, 1, None), (1, 0, -1, ((1, 0),)), (0, 1, 0, None), (1, 2, 0, ((1, 0), (0, -2), (0, -1))), (1, 0, -1, None),
+    (0, 0, 2, ()), (0, 2, 0, ((0, -1), (1, 0))), (0, 1, -1, ((0, -1),)), (1, -1, 0, None),
+    (1, -2, 0, ((-1, 0), (0, -2), (0, -1))), (0, 1, 1, ((1, 0),)), (1, 0, 1, None), (0, -2, 0, ((-1, 0), (0, 1))),
+    (1, -1, -1, ()), (1, -2, 0, None), (1, -1, 1, ()), (0, 0, 2, None), (0, -1, 1, ()), (0, -1, -1, ()),
+    (1, 1, -1, ((0, -1),)), (0, -2, 0, None), (1, 0, 2, ()), (0, -1, 1, None), (1, 3, 0, ((0, 1),)),
+    (1, 1, 1, ((1, 0),)), (0, 2, 0, None), (0, -1, -1, None), (1, 1, -1, None), (0, 1, -1, None), (1, -1, 1, None),
+    (1, 2, -1, ()), (0, 1, 1, None), (0, 3, 0, ((0, 1),)), (0, 2, -1, ((1, 0), (0, -1))), (1, 4, 0, ((0, 1),)),
+    (1, 0, 2, None), (0, 1, 2, ((3, 0),)), (0, -3, 0, ((0, 1), (-1, 0))), (1, 2, 2, ((2, 0),)), (1, 2, 0, None),
+    (0, 2, 1, ()), (1, -1, -1, None), (0, -2, 1, ((0, 1),)), (1, 1, 1, None), (1, 1, 2, ()), (1, -3, 0, ((0, -1),)),
+    (1, -3, 0, None), (1, 2, 1, ()), (1, -2, -1, ((-2, 0),)), (1, 3, 1, ((0, 1),)), (1, 4, 0, None),
+    (1, -2, 2, ((1, 0), (0, -1))), (1, -2, 2, None), (0, -3, 0, None), (0, -2, 1, None), (0, 3, 0, None),
+    (0, 2, -1, None), (1, -2, -1, None), (1, 4, 1, ((1, 0),)), (1, 3, 0, None), (0, 3, 1, ((0, 1),)), (1, 2, 1, None),
+    (0, 3, -1, ((2, 0), (1, 0))), (0, 2, 2, ()), (1, 2, 2, None), (0, -3, 1, ((0, 1),)), (0, 4, 0, ((0, 1),)),
+    (0, -2, 2, ((1, 0), (0, 1))), (1, 4, 2, ()), (1, -3, -1, ((-2, 0), (0, -1))), (1, -3, -1, None), (0, -2, 2, None),
+    (1, -2, 1, ()), (1, -2, 1, None), (0, -3, 1, None), (0, 4, 2, ()), (0, 2, 2, None), (1, 3, 2, ()),
+    (1, 4, 2, None), (1, -1, 2, ()), (1, -1, 2, None), (0, 4, 0, None), (1, 4, -1, ()), (0, 3, -1, None),
+    (1, 4, -1, None), (1, 3, 1, None), (1, -3, 1, ()), (0, 4, 2, None), (0, -2, -1, ()), (0, -2, -1, None),
+    (1, 4, 1, None), (0, 3, 2, ()), (0, 4, -1, ()), (0, 4, 1, ()), (0, -1, 2, ()), (0, -1, 2, None), (0, -3, 2, ()),
+    (1, 1, 2, None), (1, -3, 2, ()), (0, -3, -1, ()), (1, -3, 2, None), (0, -3, -1, None), (1, 2, -1, None),
+    (1, 3, -1, ()), (0, 2, 1, None), (1, 3, -1, None), (0, 1, 2, None), (0, -3, 2, None), (0, 3, 2, None),
+    (0, 4, 1, None), (0, 4, -1, None), (1, 3, 2, None), (0, 3, 1, None), (1, -3, 1, None),
+)
 
 
 def whiten(rec_ref, hi_ref, lo_ref, out_ref):
@@ -243,13 +260,16 @@
         g_ref[j, f2, 0] = own[32 * f2 : 32 * f2 + 32]
         g_ref[j, f2, 1] = other[32 * f2 : 32 * f2 + 32]
 
-    def send(u2, f2, dz, dx):
+    sign = 1 - 2 * k
+
+    def source(dz, dx):
+        return zat(-sign * dz) * NX + xat(-sign * dx)
+
+    def pass_on(u2, f2, targets):
         blk = g_ref.at[k * 32 + u2, f2]
-        remote(blk, blk, g_send, g_recv.at[k * 32 + u2, f2], device(zat(dz), xat(dx), k)).start()
-
-    def share(u2, f2):
-        blk = g_ref.at[k * 32 + u2, f2]
-        remote(blk, blk, g_send, g_recv.at[k * 32 + u2, f2], device(z, x, 1 - k)).start()
+        devices = [device(zat(sign * dz), xat(sign * dx), k) for dz, dx in targets] + [device(z, x, 1 - k)]
+        for dev in devices:
+            remote(blk, blk, g_send, g_recv.at[k * 32 + u2, f2], dev).start()
 
     def arrived(kk, u2, f2):
         blk = g_ref.at[kk * 32 + u2, f2]
@@ -265,55 +285,15 @@
         for i in range(4):
             x_ref[pl.ds(64 * i + g, 16, stride=256), :] = res[16 * i : 16 * i + 16]
 
-    for dx in (1, -1, 2):
-        send(u, 0, 0, dx)
-    for dz in (1, -1):
-        send(u, 0, dz, 0)
-    for dx in (1, -1):
-        send(u, 1, 0, dx)
-    for dz in OFF_Z:
-        send(u, 1, dz, 0)
-    share(u, 0)
-    share(u, 1)
-    todo = [(u, 0), (u, 1)]
-    for f2, dz, dx in events():
-        zs, xs = zat(dz), xat(dx)
-        b = zs * NX + xs
-        arrived(k, b, f2)
-        if f2 == 0:
-            if dz == 0:
-                send(b, 0, 1, 0)
-                send(b, 0, -1, 0)
-            elif dz in (-1, -2):
-                send(b, 0, 1, 0)
-            elif dz in (1, 2):
-                send(b, 0, -1, 0)
-            elif dz == -3:
-                @pl.when(xs % 2 == 0)
-                def _():
-                    send(b, 0, 1, 0)
-            elif dz == 3:
-                @pl.when(xs % 2 == 1)
-                def _():
-                    send(b, 0, -1, 0)
+    for f2 in range(2):
+        pass_on(u, f2, FIRST[f2])
+    for f2, dz, dx, targets in GATHER:
+        u2 = source(dz, dx)
+        if targets is None:
+            cross(u2, f2)
         else:
-            if dx == 0:
-                send(b, 1, 0, 1)
-                send(b, 1, 0, -1)
-            elif dx == -1:
-                @pl.when(zs % 2 == 0)
-                def _():
-                    send(b, 1, 0, 1)
-            elif dx == 1:
-                @pl.when(zs % 2 == 1)
-                def _():
-                    send(b, 1, 0, -1)
-        share(b, f2)
-        todo.append((b, f2))
-        if len(todo) > 3:
-            cross(*todo.pop(0))
-    for t in todo:
-        cross(*t)
+            arrived(k, u2, f2)
+            pass_on(u2, f2, targets)
     most_g = g_ref.at[pl.ds(0, NJ - 1)]
     remote(most_g, most_g, g_send, a_recv, ring_y[0]).wait_send()
     some_a.wait_send()

time: 67 us -> 62.6 us (0.934)
  Pallas kernels: 66.9 us -> 62.4 us
    pallas_call x1, Pallas kernels: 60.9 us -> 56.5 us  [body(): pl.pallas_call(exchange_kernel, out_shape=jax.ShapeDtypeStruct((16 * 256,...]
where the time goes in v3:
time: 62.6 us; the launch traced here: 62.4 us
  Pallas kernels  62.4 us (100%)
    pallas_call x1, Pallas kernels, body(): pl.pallas_call(exchange_kernel, out_shape=jax.ShapeDtypeStruct((16 * 256,...  56.5 us
    pallas_call x1, Pallas kernels, body(): pl.pallas_call(output_kernel, out_shape=jax.ShapeDtypeStruct((128 * 16, L...  5.93 us

profile of v3, /device:TPU:1, one launch (start us, length us, event | category | flops | bytes accessed | tf_op | source)
XLA Modules:
  0.0 62.4 jit_solution(2257120876867379480)
XLA Ops:
  0.0 56.5 %exchange.1.x_ref = f32[4096,128]{1,0:T(8,128)} custom-call(s32[256]{0:T(256)} %idx_ref.1, f32[256,1024]{1,0:T(8,128)} %bitcast.2, bf16[256,1024]{1,0:T(8,128)(2,1)} %constant.8.clone.hi_hbm, bf16[256,1024]{1,0:T(8,128)(2,1)} %constant.9.clone.lo_hbm), custom_call_target="tpu_custom_call" | custom-call | tf_op jit(solution)/shard_map/exchange/pallas_call | solution.py:329
  56.5 5.9 %correlate.1 = f32[2048,512]{1,0:T(8,128)} custom-call(f32[4096,128]{1,0:T(8,128)} %exchange.1.x_ref, bf16[256,512]{1,0:T(8,128)(2,1)} %constant.10.clone.hi_ref, bf16[256,512]{1,0:T(8,128)(2,1)} %constant.11.clone.lo_ref), custom_call_target="tpu_custom_call" | custom-call | tf_op jit(solution)/shard_map/correlate/pallas_call | solution.py:353

commit v4 on v3

v4 whole, which is shorter than its diff:
```python
import functools

import jax
import jax.numpy as jnp
import numpy as np
from jax import lax
from jax.experimental import pallas as pl
from jax.experimental.pallas import tpu as pltpu
from jax.sharding import PartitionSpec as P

F = 128
L = 1024
LAGS = 512
SEG = 32
water_level = 0.2
epsilon = 1e-05

NX, NZ = 4, 8
NJ = 64
ANY = pl.BlockSpec(memory_space=pl.ANY)
VMEM = pl.BlockSpec(memory_space=pltpu.VMEM)
HBM = pl.BlockSpec(memory_space=pltpu.HBM)
MESH = pl.DeviceIdType.MESH
BF = jnp.bfloat16
F32 = jnp.float32


def split_np(table):
    hi = table.astype(np.float32).astype(jnp.bfloat16)
    lo = (table - hi.astype(np.float64)).astype(np.float32).astype(jnp.bfloat16)
    return hi, lo


def forward_table():
    bins = np.arange(F) + 1
    times = np.arange(L)
    angle = 2.0 * np.pi * (bins[:, None] * times[None, :] % L) / L
    taper = 0.5 - 0.5 * np.cos(2.0 * np.pi * times / L)
    return np.concatenate((np.cos(angle) * taper, -np.sin(angle) * taper), axis=0)


def inverse_table():
    bins = np.arange(F) + 1
    shifts = np.arange(LAGS) - LAGS // 2
    angle = 2.0 * np.pi * (bins[:, None] * shifts[None, :] % L) / L
    table = np.stack((np.cos(angle), -np.sin(angle)), axis=1) / np.sqrt(SEG * F)
    return table.reshape(2, 32, 2, 2, LAGS).transpose(1, 2, 0, 3, 4).reshape(2 * F, LAGS)


def split(v):
    hi = v.astype(BF)
    return hi, (v - hi.astype(F32)).astype(BF)


def dot(a, b, ca, cb):
    return lax.dot_general(a, b, (((ca,), (cb,)), ((), ())), preferred_element_type=F32)


OFF_Z = (1, -1, 2, -2, 3, -3, 4)
FIRST = (
    ((1, 0), (-1, 0), (0, 1), (0, -1), (0, -2)),
    ((-1, 0), (2, 0), (1, 0), (0, 1), (0, -1)),
)
GATHER = (
    (1, 0, 0, None), (0, 1, 0, ((1, 0), (0, -1), (0, 1))), (0, 0, 1, ()), (1, -1, 0, ((-1, 0), (0, -1))),
    (0, 0, -1, ()), (0, -1, 0, ((-1, 0), (0, 1), (0, -1))), (1, 0, 1, ((0, 1), (-1, 0))), (1, 1, 0, ((3, 0), (0, 1))),
    (1, 0, -1, ((1, 0),)), (0, 1, 0, None), (1, 2, 0, ((1, 0), (0, -2), (0, -1))), (1, 0, -1, None), (0, 0, 2, ()),
    (0, 2, 0, ((0, -1), (1, 0))), (0, 1, -1, ((0, -1),)), (1, -1, 0, None), (1, -2, 0, ((-1, 0), (0, -2), (0, -1))),
    (0, 1, 1, ((1, 0),)), (1, 0, 1, None), (0, -2, 0, ((-1, 0), (0, 1))), (1, -1, -1, ()), (1, -1, 1, ()),
    (0, -1, 1, ()), (0, -1, -1, ()), (1, 1, -1, ((0, -1),)), (0, -2, 0, None), (1, 0, 2, ()), (1, 3, 0, ((0, 1),)),
    (1, 1, 1, ((1, 0),)), (0, 1, -1, None), (1, -1, 1, None), (1, 2, -1, ()), (0, 3, 0, ((0, 1),)),
    (0, 2, -1, ((1, 0), (0, -1))), (1, 4, 0, ((0, 1),)), (1, 0, 2, None), (0, 1, 2, ((3, 0),)),
    (0, -3, 0, ((0, 1), (-1, 0))), (1, 2, 2, ((2, 0),)), (1, 2, 0, None), (0, 2, 1, ()), (1, -1, -1, None),
    (0, -2, 1, ((0, 1),)), (1, 1, 1, None), (1, 1, 2, ()), (1, -3, 0, ((0, -1),)), (1, 2, 1, ()),
    (1, -2, -1, ((-2, 0),)), (1, 3, 1, ((0, 1),)), (1, -2, 2, ((1, 0), (0, -1))), (0, -3, 0, None),
    (1, 4, 1, ((1, 0),)), (1, 3, 0, None), (0, 3, 1, ((0, 1),)), (0, 3, -1, ((2, 0), (1, 0))), (0, 2, 2, ()),
    (0, -3, 1, ((0, 1),)), (0, 4, 0, ((0, 1),)), (0, -2, 2, ((1, 0), (0, 1))), (1, 4, 2, ()),
    (1, -3, -1, ((-2, 0), (0, -1))), (0, -2, 2, None), (1, -2, 1, ()), (1, -2, 1, None), (0, 4, 2, ()),
    (0, 2, 2, None), (1, 3, 2, ()), (1, -1, 2, ()), (0, 4, 0, None), (1, 4, -1, ()), (1, -3, 1, ()), (0, 4, 2, None),
    (0, -2, -1, ()), (0, -2, -1, None), (0, 3, 2, ()), (0, 4, -1, ()), (0, 4, 1, ()), (0, -1, 2, ()),
    (0, -1, 2, None), (0, -3, 2, ()), (1, -3, 2, ()), (0, -3, -1, ()), (0, -3, -1, None), (1, 2, -1, None),
    (1, 3, -1, ()), (0, 2, 1, None), (1, 3, -1, None), (0, 1, 2, None), (0, -3, 2, None), (0, 4, 1, None),
    (0, 4, -1, None), (1, 3, 2, None), (0, 3, 1, None), (1, -3, 1, None),
)


def whiten(rec_ref, hi_ref, lo_ref, out_ref):
    rec_hi, rec_lo = split(rec_ref[...])
    spec = dot(hi_ref[...], rec_hi, 1, 1) + dot(hi_ref[...], rec_lo, 1, 1) + dot(lo_ref[...], rec_hi, 1, 1)
    re, im = spec[:F], spec[F:]
    mag = jnp.sqrt(re * re + im * im)
    zeros = jnp.zeros((2, mag.shape[1]), F32)
    pad = jnp.concatenate((zeros, mag, zeros), axis=0)
    smooth = pad[0:F]
    for off in range(1, 5):
        smooth = smooth + pad[off : off + F]
    mean = jnp.sum(mag, axis=0, keepdims=True) * (1.0 / F)
    divisor = smooth / 5.0 + water_level * mean + epsilon
    for q, part in enumerate((re, im)):
        white = part / divisor
        for s_hi in range(2):
            out_ref[pl.ds(2 * q + s_hi, F, stride=4), :] = white[:, 128 * s_hi : 128 * (s_hi + 1)]


def swap(v, bit, lane):
    step = 1 << bit
    low = (lane & step) == 0
    v = list(v)
    for i in range(len(v)):
        if i & step:
            continue
        a, b = v[i], v[i + step]
        v[i] = jnp.where(low, a, pltpu.roll(b, step, 1))
        v[i + step] = jnp.where(low, pltpu.roll(a, 128 - step, 1), b)
    return v


def lanes():
    return lax.broadcasted_iota(jnp.int32, (16, 128), 1)


def receivers_first(ref, mid_ref, side):
    v = []
    for e in range(4):
        t = ref[pl.ds(e, F, stride=4), :].T
        v += [t[16 * i : 16 * i + 16] for i in range(8)]
    for bit in range(5):
        v = swap(v, bit, lanes())
    for i in range(32):
        mid_ref[side, i] = v[i]


def receivers_last(mid_ref, lhs_ref):
    lane = lanes()
    first = (lane & 16) == 0
    low = (lane & 32) == 0
    row8 = lax.broadcasted_iota(jnp.int32, (8, 128), 0)
    lane8 = lax.broadcasted_iota(jnp.int32, (8, 128), 1)
    imag = (row8 & 1) == 1
    same = ((row8 >> 1) & 1) == (lane8 >> 6)
    keep = [same & ((row8 >> 2) == f2) for f2 in range(2)]
    for i in range(32):
        a, b = mid_ref[0, i], mid_ref[1, i]
        pair = (jnp.where(low, a, pltpu.roll(b, 32, 1)), jnp.where(low, pltpu.roll(a, 96, 1), b))
        for half in range(2):
            g = 32 * half + i
            u, f2 = g // 2, g % 2
            re = pair[half]
            im = jnp.where(first, pltpu.roll(re, 112, 1), -pltpu.roll(re, 16, 1))
            rows = []
            for c in range(16):
                v = jnp.where(
                    imag, jnp.broadcast_to(im[c : c + 1], (8, 128)), jnp.broadcast_to(re[c : c + 1], (8, 128))
                )
                rows.append(jnp.where(keep[f2], v, 0.0))
            hi, lo = split(jnp.concatenate(rows, axis=0))
            lhs_ref[u, 0:128, 128 * f2 : 128 * f2 + 128] = hi
            lhs_ref[u, 128:256, 128 * f2 : 128 * f2 + 128] = lo


def exchange_kernel(idx_hbm, rec_hbm, hi_hbm, lo_hbm, x_ref, idx_ref, rec_ref, hi_ref, lo_ref, w_ref, wo_ref, z_ref, a_ref,
                    gm_ref, pick_ref, y_ref, g_ref, mid_ref, lhs_ref,
                    load, z_send, z_recv, a_send, a_recv, y_send, y_recv, wo_send, wo_recv, g_send, g_recv):
    h = lax.axis_index("half")
    s = lax.axis_index("shard")
    yh, u, k = s // NJ, (s % NJ) // 2, s % 2
    z, x = u // NX, u % NX
    j = k * 32 + u

    def device(zz, xx, kk):
        return (h, yh * NJ + (zz * NX + xx) * 2 + kk)

    def zat(d):
        return (z + d + NZ) % NZ

    def xat(d):
        return (x + d + NX) % NX

    def remote(src, dst, ssem, rsem, dev):
        return pltpu.make_async_remote_copy(
            src_ref=src, dst_ref=dst, send_sem=ssem, recv_sem=rsem, device_id=dev, device_id_type=MESH
        )

    plane = [(xat(d), kk) for d in (0, 1, -1, 2) for kk in (k, 1 - k)][1:]
    ring_y = [(h, (1 - yh) * NJ + s % NJ), (1 - h, s), (1 - h, (1 - yh) * NJ + s % NJ)]
    barrier = pltpu.get_barrier_semaphore()
    for dev in [device(zat(d), x, k) for d in OFF_Z] + [device(z, *p) for p in plane] + ring_y:
        pl.semaphore_signal(barrier, inc=1, device_id=dev, device_id_type=MESH)
    loads = [
        pltpu.make_async_copy(a, b, load.at[i])
        for i, (a, b) in enumerate(((rec_hbm, rec_ref), (hi_hbm, hi_ref), (lo_hbm, lo_ref), (idx_hbm, idx_ref)))
    ]
    for c in loads:
        c.start()
    for c in loads:
        c.wait()
    whiten(rec_ref, hi_ref, lo_ref, w_ref)
    pl.semaphore_wait(barrier, 17)

    def rows(kk, zz, n):
        return pl.ds(pl.multiple_of((kk * 32 + zz * NX) * 8, 8), n)

    for d in OFF_Z:
        for kk in range(2):
            remote(
                w_ref.at[rows(kk, zat(d), 32)], z_ref.at[kk, z], z_send, z_recv.at[kk, z], device(zat(d), x, k)
            ).start()
    wo = remote(w_ref, wo_ref, wo_send, wo_recv, ring_y[1])
    wo.start()
    for kk in range(2):
        z_ref[kk, z] = w_ref[rows(kk, z, 32), :]
    receivers_first(w_ref, mid_ref, 0)
    for d in (0,) + OFF_Z:
        zs = zat(d)
        if d:
            for kk in range(2):
                remote(z_ref.at[kk, zs], z_ref.at[kk, zs], z_send, z_recv.at[kk, zs], ring_y[0]).wait_recv()
        mine = k * 32 + zs * NX + x
        for xx, kk in plane:
            src = z_ref.at[kk, zs, pl.ds(pl.multiple_of(xx * 8, 8), 8)]
            remote(src, a_ref.at[mine], a_send, a_recv, device(z, xx, kk)).start()
        a_ref[mine] = z_ref[k, zs, pl.ds(pl.multiple_of(x * 8, 8), 8), :]
    wo.wait()
    receivers_first(wo_ref, mid_ref, 1)
    receivers_last(mid_ref, lhs_ref)
    some_a = remote(a_ref.at[pl.ds(0, 56)], a_ref.at[pl.ds(0, 56)], a_send, a_recv, ring_y[0])
    some_a.wait_recv()

    lane_c = lax.broadcasted_iota(jnp.int32, (8, 128), 1) & 15

    row = lax.broadcasted_iota(jnp.int32, (8, 128), 0)
    fold = jnp.where((lax.broadcasted_iota(jnp.int32, (8, 128), 1) >> 4) == row, 1.0, 0.0).astype(BF)
    trades = [
        remote(pick_ref.at[1], y_ref.at[0], y_send.at[0], y_recv.at[0], ring_y[0]),
        remote(pick_ref.at[0], y_ref.at[1], y_send.at[1], y_recv.at[1], ring_y[1]),
        remote(pick_ref.at[0], y_ref.at[2], y_send.at[2], y_recv.at[2], ring_y[2]),
    ]
    for own in range(2):
        base = (h if own else 1 - h) * 128

        def pick(n, carry):
            q = idx_ref[base + n]
            p = q >> 4
            c = jnp.where((p >> 6) == yh, q & 15, 99)
            v = jnp.where(lane_c == c, a_ref[(p & 1) * 32 + ((p & 63) >> 1)], 0.0)
            gm_ref[own, pl.ds(n, 8, stride=128), :] = v
            return carry

        lax.fori_loop(0, 128, pick, 0, unroll=16)
        for e in range(8):
            v = gm_ref[own, 128 * e : 128 * (e + 1), :]
            hi = v.astype(BF)
            rest = v - hi.astype(F32)
            mid = rest.astype(BF)
            lo = (rest - mid.astype(F32)).astype(BF)
            pick_ref[own, 8 * e : 8 * (e + 1), :] = dot(fold, hi, 1, 1) + dot(fold, mid, 1, 1) + dot(fold, lo, 1, 1)
        if own:
            trades[0].start()
        else:
            trades[2].start()
            trades[1].start()
    for t in trades:
        t.wait()
    own = pick_ref[1] + y_ref[0]
    other = y_ref[1] + y_ref[2]
    for f2 in range(2):
        g_ref[j, f2, 0] = own[32 * f2 : 32 * f2 + 32]
        g_ref[j, f2, 1] = other[32 * f2 : 32 * f2 + 32]

    sign = 1 - 2 * k

    def source(dz, dx):
        return zat(-sign * dz) * NX + xat(-sign * dx)

    def pass_on(u2, f2, targets):
        blk = g_ref.at[k * 32 + u2, f2]
        devices = [device(zat(sign * dz), xat(sign * dx), k) for dz, dx in targets] + [device(z, x, 1 - k)]
        for dev in devices:
            remote(blk, blk, g_send, g_recv.at[k * 32 + u2, f2], dev).start()

    def arrived(kk, u2, f2):
        blk = g_ref.at[kk * 32 + u2, f2]
        remote(blk, blk, g_send, g_recv.at[kk * 32 + u2, f2], ring_y[0]).wait_recv()

    low_n = [(lax.broadcasted_iota(jnp.int32, (8, 128), 1) & (1 << bit)) == 0 for bit in range(4)]

    def cross(u2):
        blocks = []
        for f2 in range(2):
            arrived(1 - k, u2, f2)
            blocks += [g_ref[u2, f2].reshape(64, 128), g_ref[32 + u2, f2].reshape(64, 128)]
        hi, lo = split(jnp.concatenate(blocks, axis=0))
        res = dot(lhs_ref[u2], jnp.concatenate((hi, lo), axis=1), 1, 0)
        res = res[:128, :128] + (res[:128, 128:] + res[128:, :128])
        v = [res[8 * c : 8 * c + 8] for c in range(16)]
        for bit in range(4):
            step = 1 << bit
            for i in range(16):
                if i & step:
                    continue
                a, b = v[i], v[i + step]
                v[i] = jnp.where(low_n[bit], a, pltpu.roll(b, step, 1))
                v[i + step] = jnp.where(low_n[bit], pltpu.roll(a, 128 - step, 1), b)
        at = pl.ds(pl.multiple_of(8 * u2, 8), 8)
        for i in range(16):
            x_ref[i, at, :] = v[i]

    for f2 in range(2):
        pass_on(u, f2, FIRST[f2])
    for f2, dz, dx, targets in GATHER:
        u2 = source(dz, dx)
        if targets is None:
            cross(u2)
        else:
            arrived(k, u2, f2)
            pass_on(u2, f2, targets)
    most_g = g_ref.at[pl.ds(0, NJ - 1)]
    remote(most_g, most_g, g_send, a_recv, ring_y[0]).wait_send()
    some_a.wait_send()
    sent_z = w_ref.at[pl.ds(0, 448)]
    remote(sent_z, sent_z, z_send, a_recv, ring_y[0]).wait_send()


def output_kernel(x_ref, hi_hbm, lo_hbm, out_ref, hi_ref, lo_ref, stage_ref, load, sem):
    loads = [
        pltpu.make_async_copy(hi_hbm, hi_ref, load.at[0]),
        pltpu.make_async_copy(lo_hbm, lo_ref, load.at[1]),
    ]
    for c in loads:
        c.start()
    copies = []
    for m in range(0, 16, 2):
        parts = [split(x_ref[i].T) for i in (m, m + 1)]
        hi = jnp.concatenate([p[0] for p in parts], axis=0)
        lo = jnp.concatenate([p[1] for p in parts], axis=0)
        if m == 0:
            for c in loads:
                c.wait()
        both = dot(jnp.concatenate((hi, lo), axis=0), hi_ref[...], 1, 0)
        res = both[:256] + (both[256:] + dot(hi, lo_ref[...], 1, 0))
        for i in range(2):
            stage_ref[m + i] = res[128 * i : 128 * i + 128].reshape(8, 16, LAGS)
            copy = pltpu.make_async_copy(stage_ref.at[m + i], out_ref.at[:, m + i], sem.at[m + i])
            copy.start()
            copies.append(copy)
    for copy in copies:
        copy.wait()


def body(recording, source_channels):
    fwd_hi, fwd_lo = (jnp.asarray(t) for t in split_np(forward_table()))
    inv_hi, inv_lo = (jnp.asarray(t) for t in split_np(inverse_table()))
    dma = pltpu.SemaphoreType.DMA
    cross = pl.pallas_call(
        exchange_kernel,
        out_shape=pltpu.VMEM((16, 256, 128), F32),
        in_specs=[HBM] * 4,
        out_specs=VMEM,
        scratch_shapes=[
            pltpu.SMEM((256,), jnp.int32),
            pltpu.VMEM((256, L), F32),
            pltpu.VMEM((256, L), BF),
            pltpu.VMEM((256, L), BF),
            pltpu.VMEM((512, 128), F32),
            pltpu.VMEM((512, 128), F32),
            pltpu.VMEM((2, NZ, 32, 128), F32),
            pltpu.VMEM((NJ, 8, 128), F32),
            pltpu.VMEM((2, 1024, 128), F32),
            pltpu.VMEM((2, 64, 128), F32),
            pltpu.VMEM((3, 64, 128), F32),
            pltpu.VMEM((NJ, 2, 2, 32, 128), F32),
            pltpu.VMEM((2, 32, 16, 128), F32),
            pltpu.VMEM((32, 256, 256), BF),
            dma((4,)), dma, dma((2, NZ)), dma, dma, dma((3,)), dma((3,)), dma, dma, dma, dma((NJ, 2)),
        ],
        compiler_params=pltpu.CompilerParams(collective_id=0, has_side_effects=True),
        name="exchange",
    )(source_channels, recording.reshape(256, L), fwd_hi, fwd_lo)
    out = pl.pallas_call(
        output_kernel,
        out_shape=jax.ShapeDtypeStruct((8, 16, 16, LAGS), F32),
        in_specs=[VMEM, ANY, ANY],
        out_specs=ANY,
        scratch_shapes=[
            pltpu.VMEM((256, LAGS), BF),
            pltpu.VMEM((256, LAGS), BF),
            pltpu.VMEM((16, 8, 16, LAGS), F32),
            dma((2,)),
            dma((16,)),
        ],
        compiler_params=pltpu.CompilerParams(vmem_limit_bytes=24 << 20),
        name="correlate",
    )(cross, inv_hi, inv_lo)
    return out.reshape(128, 16, LAGS)


def solution(mesh):
    return jax.shard_map(
        body,
        mesh=mesh,
        in_specs=(P("half", "shard", None), P()),
        out_specs=P("half", "shard", None),
        check_vma=False,
    )
```

time: 62.6 us -> 59.9 us (0.957)
  Pallas kernels: 62.4 us -> 59.6 us
    pallas_call x2, Pallas kernels: 62.4 us -> 59.6 us  [the longest x1 56.8 us: body(): pl.pallas_call(exchange_kernel, out_shape=pltpu.VMEM((16, 256, 128), F32)...]
where the time goes in v4:
time: 59.9 us; the launch traced here: 59.8 us
  Pallas kernels  59.6 us (99%)
    pallas_call x1, Pallas kernels, body(): pl.pallas_call(exchange_kernel, out_shape=pltpu.VMEM((16, 256, 128), F32)...  56.8 us
    pallas_call x1, Pallas kernels, body(): pl.pallas_call(output_kernel, out_shape=jax.ShapeDtypeStruct((8, 16, 16,...  2.89 us

profile of v4, /device:TPU:1, one launch (start us, length us, event | category | flops | bytes accessed | tf_op | source)
XLA Modules:
  0.0 59.8 jit_solution(6844206408375417627)
XLA Ops:
  0.0 0.0 copy-start
  0.0 0.0 copy-start.1
  0.0 56.8 %exchange.1.x_ref = f32[16,256,128]{2,1,0:T(8,128)S(1)} custom-call(s32[256]{0:T(256)} %idx_hbm.1, f32[256,1024]{1,0:T(8,128)} %bitcast.2, bf16[256,1024]{1,0:T(8,128)(2,1)} %constant.8.clone.hi_hbm, bf16[256,1024]{1,0:T(8,128)(2,1)} %constant.9.clone.lo_hbm), custom_call_target="tpu_custom_call" | custom-call | tf_op jit(solution)/shard_map/exchange/pallas_call | solution.py:354
  56.8 0.0 copy-done
  56.8 0.0 copy-done.1
  56.8 2.9 %correlate.1 = f32[8,16,16,512]{3,2,1,0:T(8,128)} custom-call(f32[16,256,128]{2,1,0:T(8,128)S(1)} %exchange.1.x_ref, bf16[256,512]{1,0:T(8,128)(2,1)S(1)} %copy-done.1, bf16[256,512]{1,0:T(8,128)(2,1)S(1)} %copy-done), custom_call_target="tpu_custom_call" | custom-call | tf_op jit(solution)/shard_map/correlate/pallas_call | solution.py:379
Async XLA Ops:
  0.0 56.8 %copy-start = (bf16[256,512]{1,0:T(8,128)(2,1)S(1)}, bf16[256,512]{1,0:T(8,128)(2,1)}, u32[]{:S(2)}) copy-start(bf16[256,512]{1,0:T(8,128)(2,1)} %constant.11.clone.lo_hbm) | copy-start | bytes 786436
  0.0 56.8 %copy-start.1 = (bf16[256,512]{1,0:T(8,128)(2,1)S(1)}, bf16[256,512]{1,0:T(8,128)(2,1)}, u32[]{:S(2)}) copy-start(bf16[256,512]{1,0:T(8,128)(2,1)} %constant.10.clone.hi_hbm) | copy-start | bytes 786436

commit v5 on v4

--- a/solution.py
+++ b/solution.py
@@ -238,22 +238,27 @@
     for own in range(2):
         base = (h if own else 1 - h) * 128
 
-        def pick(n, carry):
-            q = idx_ref[base + n]
+        def pick(i, carry):
+            q = idx_ref[base + (i & 15) * 8 + (i >> 4)]
             p = q >> 4
             c = jnp.where((p >> 6) == yh, q & 15, 99)
             v = jnp.where(lane_c == c, a_ref[(p & 1) * 32 + ((p & 63) >> 1)], 0.0)
-            gm_ref[own, pl.ds(n, 8, stride=128), :] = v
+            gm_ref[own, pl.ds(pl.multiple_of(8 * i, 8), 8), :] = v
             return carry
 
         lax.fori_loop(0, 128, pick, 0, unroll=16)
-        for e in range(8):
-            v = gm_ref[own, 128 * e : 128 * (e + 1), :]
+        got = []
+        for t in range(8):
+            v = gm_ref[own, 128 * t : 128 * (t + 1), :]
             hi = v.astype(BF)
             rest = v - hi.astype(F32)
             mid = rest.astype(BF)
             lo = (rest - mid.astype(F32)).astype(BF)
-            pick_ref[own, 8 * e : 8 * (e + 1), :] = dot(fold, hi, 1, 1) + dot(fold, mid, 1, 1) + dot(fold, lo, 1, 1)
+            got.append(dot(fold, hi, 1, 1) + dot(fold, mid, 1, 1) + dot(fold, lo, 1, 1))
+        for bit in range(3):
+            got = swap(got, bit, lax.broadcasted_iota(jnp.int32, (8, 128), 1))
+        for e in range(8):
+            pick_ref[own, 8 * e : 8 * (e + 1), :] = got[e]
         if own:
             trades[0].start()
         else:
@@ -282,35 +287,31 @@
         blk = g_ref.at[kk * 32 + u2, f2]
         remote(blk, blk, g_send, g_recv.at[kk * 32 + u2, f2], ring_y[0]).wait_recv()
 
-    low_n = [(lax.broadcasted_iota(jnp.int32, (8, 128), 1) & (1 << bit)) == 0 for bit in range(4)]
-
-    def cross(u2):
-        blocks = []
-        for f2 in range(2):
-            arrived(1 - k, u2, f2)
-            blocks += [g_ref[u2, f2].reshape(64, 128), g_ref[32 + u2, f2].reshape(64, 128)]
-        hi, lo = split(jnp.concatenate(blocks, axis=0))
-        res = dot(lhs_ref[u2], jnp.concatenate((hi, lo), axis=1), 1, 0)
-        res = res[:128, :128] + (res[:128, 128:] + res[128:, :128])
-        v = [res[8 * c : 8 * c + 8] for c in range(16)]
-        for bit in range(4):
-            step = 1 << bit
-            for i in range(16):
-                if i & step:
-                    continue
-                a, b = v[i], v[i + step]
-                v[i] = jnp.where(low_n[bit], a, pltpu.roll(b, step, 1))
-                v[i + step] = jnp.where(low_n[bit], pltpu.roll(a, 128 - step, 1), b)
-        at = pl.ds(pl.multiple_of(8 * u2, 8), 8)
-        for i in range(16):
-            x_ref[i, at, :] = v[i]
-
+    def cross(*us):
+        for u2 in us:
+            for f2 in range(2):
+                arrived(1 - k, u2, f2)
+        for u2 in us:
+            blocks = []
+            for f2 in range(2):
+                blocks += [g_ref[u2, f2].reshape(64, 128), g_ref[32 + u2, f2].reshape(64, 128)]
+            hi, lo = split(jnp.concatenate(blocks, axis=0))
+            res = dot(lhs_ref[u2], jnp.concatenate((hi, lo), axis=1), 1, 0)
+            res = res[:128, :128] + (res[:128, 128:] + res[128:, :128])
+            at = pl.ds(pl.multiple_of(8 * u2, 8), 8)
+            for c in range(16):
+                x_ref[c, at, :] = res[8 * c : 8 * c + 8]
+
+    ready = []
     for f2 in range(2):
         pass_on(u, f2, FIRST[f2])
     for f2, dz, dx, targets in GATHER:
         u2 = source(dz, dx)
         if targets is None:
-            cross(u2)
+            ready.append(u2)
+            if len(ready) == 2:
+                cross(*ready)
+                ready = []
         else:
             arrived(k, u2, f2)
             pass_on(u2, f2, targets)
@@ -321,28 +322,30 @@
     remote(sent_z, sent_z, z_send, a_recv, ring_y[0]).wait_send()
 
 
-def output_kernel(x_ref, hi_hbm, lo_hbm, out_ref, hi_ref, lo_ref, stage_ref, load, sem):
+def output_kernel(x_ref, hi_hbm, lo_hbm, out_ref, hi_ref, lo_ref, mix_ref, stage_ref, load, sem):
     loads = [
         pltpu.make_async_copy(hi_hbm, hi_ref, load.at[0]),
         pltpu.make_async_copy(lo_hbm, lo_ref, load.at[1]),
     ]
     for c in loads:
         c.start()
+    for c in range(16):
+        t = x_ref[c].T
+        for half in range(2):
+            mix_ref[half, pl.ds(c, 128, stride=16), :] = t[:, 128 * half : 128 * half + 128]
     copies = []
-    for m in range(0, 16, 2):
-        parts = [split(x_ref[i].T) for i in (m, m + 1)]
-        hi = jnp.concatenate([p[0] for p in parts], axis=0)
-        lo = jnp.concatenate([p[1] for p in parts], axis=0)
+    for m in range(8):
+        parts = [split(mix_ref[half, 256 * m : 256 * m + 256, :]) for half in range(2)]
+        hi = jnp.concatenate([p[0] for p in parts], axis=1)
+        lo = jnp.concatenate([p[1] for p in parts], axis=1)
         if m == 0:
             for c in loads:
                 c.wait()
         both = dot(jnp.concatenate((hi, lo), axis=0), hi_ref[...], 1, 0)
-        res = both[:256] + (both[256:] + dot(hi, lo_ref[...], 1, 0))
-        for i in range(2):
-            stage_ref[m + i] = res[128 * i : 128 * i + 128].reshape(8, 16, LAGS)
-            copy = pltpu.make_async_copy(stage_ref.at[m + i], out_ref.at[:, m + i], sem.at[m + i])
-            copy.start()
-            copies.append(copy)
+        stage_ref[m] = both[:256] + (both[256:] + dot(hi, lo_ref[...], 1, 0))
+        copy = pltpu.make_async_copy(stage_ref.at[m], out_ref.at[pl.ds(256 * m, 256)], sem.at[m])
+        copy.start()
+        copies.append(copy)
     for copy in copies:
         copy.wait()
 
@@ -378,15 +381,16 @@
     )(source_channels, recording.reshape(256, L), fwd_hi, fwd_lo)
     out = pl.pallas_call(
         output_kernel,
-        out_shape=jax.ShapeDtypeStruct((8, 16, 16, LAGS), F32),
+        out_shape=jax.ShapeDtypeStruct((2048, LAGS), F32),
         in_specs=[VMEM, ANY, ANY],
         out_specs=ANY,
         scratch_shapes=[
             pltpu.VMEM((256, LAGS), BF),
             pltpu.VMEM((256, LAGS), BF),
-            pltpu.VMEM((16, 8, 16, LAGS), F32),
+            pltpu.VMEM((2, 2048, 128), F32),
+            pltpu.VMEM((8, 256, LAGS), F32),
             dma((2,)),
-            dma((16,)),
+            dma((8,)),
         ],
         compiler_params=pltpu.CompilerParams(vmem_limit_bytes=24 << 20),
         name="correlate",

time: 59.9 us -> 56.6 us (0.945)
  Pallas kernels: 59.6 us -> 56.4 us
    pallas_call x1, Pallas kernels: 56.8 us -> 52.5 us  [body(): pl.pallas_call(exchange_kernel, out_shape=pltpu.VMEM((16, 256, 128), F32)...]
    pallas_call x1, Pallas kernels: 2.89 us -> 3.91 us  [body(): pl.pallas_call(output_kernel, out_shape=jax.ShapeDtypeStruct((2048, LAGS)...]
where the time goes in v5:
time: 56.6 us; the launch traced here: 56.5 us
  Pallas kernels  56.4 us (100%)
    pallas_call x1, Pallas kernels, body(): pl.pallas_call(exchange_kernel, out_shape=pltpu.VMEM((16, 256, 128), F32)...  52.5 us
    pallas_call x1, Pallas kernels, body(): pl.pallas_call(output_kernel, out_shape=jax.ShapeDtypeStruct((2048, LAGS)...  3.91 us

profile of v5, /device:TPU:1, one launch (start us, length us, event | category | flops | bytes accessed | tf_op | source)
XLA Modules:
  0.0 56.5 jit_solution(12365737718703484747)
XLA Ops:
  0.0 0.0 copy-start
  0.0 0.0 copy-start.1
  0.0 52.5 %exchange.1.x_ref = f32[16,256,128]{2,1,0:T(8,128)S(1)} custom-call(s32[256]{0:T(256)} %idx_hbm.1, f32[256,1024]{1,0:T(8,128)} %bitcast.2, bf16[256,1024]{1,0:T(8,128)(2,1)} %constant.8.clone.hi_hbm, bf16[256,1024]{1,0:T(8,128)(2,1)} %constant.9.clone.lo_hbm), custom_call_target="tpu_custom_call" | custom-call | tf_op jit(solution)/shard_map/exchange/pallas_call | solution.py:357
  52.5 0.0 copy-done
  52.6 0.0 copy-done.1
  52.6 3.9 %correlate.1 = f32[2048,512]{1,0:T(8,128)} custom-call(f32[16,256,128]{2,1,0:T(8,128)S(1)} %exchange.1.x_ref, bf16[256,512]{1,0:T(8,128)(2,1)S(1)} %copy-done.1, bf16[256,512]{1,0:T(8,128)(2,1)S(1)} %copy-done), custom_call_target="tpu_custom_call" | custom-call | tf_op jit(solution)/shard_map/correlate/pallas_call | solution.py:382
Async XLA Ops:
  0.0 52.5 %copy-start = (bf16[256,512]{1,0:T(8,128)(2,1)S(1)}, bf16[256,512]{1,0:T(8,128)(2,1)}, u32[]{:S(2)}) copy-start(bf16[256,512]{1,0:T(8,128)(2,1)} %constant.11.clone.lo_hbm) | copy-start | bytes 786436
  0.0 52.6 %copy-start.1 = (bf16[256,512]{1,0:T(8,128)(2,1)S(1)}, bf16[256,512]{1,0:T(8,128)(2,1)}, u32[]{:S(2)}) copy-start(bf16[256,512]{1,0:T(8,128)(2,1)} %constant.10.clone.hi_hbm) | copy-start | bytes 786436

commit v6 on v5

--- a/solution.py
+++ b/solution.py
@@ -58,29 +58,32 @@
 
 OFF_Z = (1, -1, 2, -2, 3, -3, 4)
 FIRST = (
-    ((1, 0), (-1, 0), (0, 1), (0, -1), (0, -2)),
-    ((-1, 0), (2, 0), (1, 0), (0, 1), (0, -1)),
+    ((-1, 0), (2, 0), (0, -2), (4, 0)),
+    ((0, 1), (0, -1), (2, 0)),
 )
 GATHER = (
-    (1, 0, 0, None), (0, 1, 0, ((1, 0), (0, -1), (0, 1))), (0, 0, 1, ()), (1, -1, 0, ((-1, 0), (0, -1))),
-    (0, 0, -1, ()), (0, -1, 0, ((-1, 0), (0, 1), (0, -1))), (1, 0, 1, ((0, 1), (-1, 0))), (1, 1, 0, ((3, 0), (0, 1))),
-    (1, 0, -1, ((1, 0),)), (0, 1, 0, None), (1, 2, 0, ((1, 0), (0, -2), (0, -1))), (1, 0, -1, None), (0, 0, 2, ()),
-    (0, 2, 0, ((0, -1), (1, 0))), (0, 1, -1, ((0, -1),)), (1, -1, 0, None), (1, -2, 0, ((-1, 0), (0, -2), (0, -1))),
-    (0, 1, 1, ((1, 0),)), (1, 0, 1, None), (0, -2, 0, ((-1, 0), (0, 1))), (1, -1, -1, ()), (1, -1, 1, ()),
-    (0, -1, 1, ()), (0, -1, -1, ()), (1, 1, -1, ((0, -1),)), (0, -2, 0, None), (1, 0, 2, ()), (1, 3, 0, ((0, 1),)),
-    (1, 1, 1, ((1, 0),)), (0, 1, -1, None), (1, -1, 1, None), (1, 2, -1, ()), (0, 3, 0, ((0, 1),)),
-    (0, 2, -1, ((1, 0), (0, -1))), (1, 4, 0, ((0, 1),)), (1, 0, 2, None), (0, 1, 2, ((3, 0),)),
-    (0, -3, 0, ((0, 1), (-1, 0))), (1, 2, 2, ((2, 0),)), (1, 2, 0, None), (0, 2, 1, ()), (1, -1, -1, None),
-    (0, -2, 1, ((0, 1),)), (1, 1, 1, None), (1, 1, 2, ()), (1, -3, 0, ((0, -1),)), (1, 2, 1, ()),
-    (1, -2, -1, ((-2, 0),)), (1, 3, 1, ((0, 1),)), (1, -2, 2, ((1, 0), (0, -1))), (0, -3, 0, None),
-    (1, 4, 1, ((1, 0),)), (1, 3, 0, None), (0, 3, 1, ((0, 1),)), (0, 3, -1, ((2, 0), (1, 0))), (0, 2, 2, ()),
-    (0, -3, 1, ((0, 1),)), (0, 4, 0, ((0, 1),)), (0, -2, 2, ((1, 0), (0, 1))), (1, 4, 2, ()),
-    (1, -3, -1, ((-2, 0), (0, -1))), (0, -2, 2, None), (1, -2, 1, ()), (1, -2, 1, None), (0, 4, 2, ()),
-    (0, 2, 2, None), (1, 3, 2, ()), (1, -1, 2, ()), (0, 4, 0, None), (1, 4, -1, ()), (1, -3, 1, ()), (0, 4, 2, None),
-    (0, -2, -1, ()), (0, -2, -1, None), (0, 3, 2, ()), (0, 4, -1, ()), (0, 4, 1, ()), (0, -1, 2, ()),
-    (0, -1, 2, None), (0, -3, 2, ()), (1, -3, 2, ()), (0, -3, -1, ()), (0, -3, -1, None), (1, 2, -1, None),
-    (1, 3, -1, ()), (0, 2, 1, None), (1, 3, -1, None), (0, 1, 2, None), (0, -3, 2, None), (0, 4, 1, None),
-    (0, 4, -1, None), (1, 3, 2, None), (0, 3, 1, None), (1, -3, 1, None),
+    (0, 0, 0, None, 0), (0, -1, 0, ((0, 1), (-1, 0), (0, -1)), 1), (1, 0, 1, ((-3, 0), (1, 0)), 0),
+    (1, 0, -1, ((0, -1),), 0), (0, 0, 2, ((1, 0), (0, 1)), 0), (0, 2, 0, ((0, -2), (0, 1), (0, -1)), 0),
+    (1, 2, 0, ((1, 0),), 0), (0, -1, 1, ((0, 1), (1, 0)), 0), (0, -2, 0, ((-1, 0), (0, 1)), 1),
+    (0, -1, -1, ((-1, 0),), 0), (1, 0, 2, ((-1, 0),), 0), (1, -1, 0, (), 0), (1, 1, 1, ((1, 0), (0, -1)), 0),
+    (0, 0, -1, (), 0), (0, 4, 0, ((0, 1), (0, -1)), 1), (0, 0, 2, None, 0), (0, 2, 1, ((1, 0),), 0),
+    (0, 1, 2, ((0, 1), (0, -1)), 1), (0, 2, -1, (), 1), (1, 3, 0, ((0, -1), (0, 1)), 0),
+    (0, 2, 2, ((1, 0), (2, 0)), 1), (1, -3, 1, ((0, 1), (1, 0), (0, -1)), 0), (0, -1, 2, ((-1, 0),), 0),
+    (0, 0, 1, (), 0), (0, 0, 1, None, 0), (0, -2, 1, (), 0), (0, -2, -1, (), 1), (1, 1, 0, (), 0), (1, -2, 0, (), 0),
+    (0, -3, 0, ((-2, 0), (0, -1)), 0), (0, 4, 1, ((1, 0),), 0), (1, -1, 2, ((0, -1), (0, 1)), 0), (0, 0, -1, None, 0),
+    (0, 4, -1, ((-1, 0),), 1), (1, 2, 1, ((2, 0),), 0), (1, 4, 0, (), 0), (0, 1, -1, ((0, 1),), 1), (0, 3, 1, (), 0),
+    (0, 1, 1, (), 0), (0, 3, 2, (), 0), (1, 1, 2, (), 0), (0, 1, 2, None, 0), (1, 3, -1, ((0, -1),), 0),
+    (1, 3, 1, (), 0), (1, -2, 1, ((0, 1),), 0), (1, 2, -1, (), 0), (1, -3, 2, ((0, 1), (-1, 0)), 0),
+    (0, -2, 2, ((-1, 0),), 0), (1, -3, 0, (), 0), (0, 4, 2, (), 0), (1, 2, 2, (), 0), (0, -3, -1, (), 0),
+    (1, -1, 1, (), 0), (0, 2, 0, None, 0), (0, 4, 0, None, 0), (0, 2, -1, None, 0), (1, -2, -1, (), 0),
+    (1, -1, -1, (), 0), (0, -1, -1, None, 0), (0, -3, 1, (), 0), (0, 1, 0, (), 0), (0, -1, 2, None, 0),
+    (0, 1, 0, None, 0), (0, -2, 1, None, 0), (0, 3, -1, (), 0), (1, 4, -1, (), 0), (0, 3, 0, (), 0), (1, 3, 2, (), 0),
+    (0, 3, 0, None, 0), (1, 4, 1, (), 0), (1, -2, 2, (), 0), (0, 1, 1, None, 0), (1, 1, -1, (), 0),
+    (1, -3, -1, (), 0), (1, 4, 2, (), 0), (0, -3, -1, None, 0), (0, -3, 2, (), 0), (0, -3, 1, None, 0),
+    (0, 3, -1, None, 0), (0, -2, 2, None, 0), (0, -1, 0, None, 0), (0, -3, 0, None, 0), (0, -3, 2, None, 0),
+    (0, 4, -1, None, 0), (0, 2, 1, None, 0), (0, 4, 1, None, 0), (0, 2, 2, None, 0), (0, 3, 1, None, 0),
+    (0, 4, 2, None, 0), (0, -1, 1, None, 0), (0, 3, 2, None, 0), (0, -2, 0, None, 0), (0, -2, -1, None, 0),
+    (0, 1, -1, None, 0),
 )
 
 
@@ -277,9 +280,11 @@
     def source(dz, dx):
         return zat(-sign * dz) * NX + xat(-sign * dx)
 
-    def pass_on(u2, f2, targets):
+    def pass_on(u2, f2, targets, over_y=False):
         blk = g_ref.at[k * 32 + u2, f2]
         devices = [device(zat(sign * dz), xat(sign * dx), k) for dz, dx in targets] + [device(z, x, 1 - k)]
+        if over_y:
+            devices.append(ring_y[0])
         for dev in devices:
             remote(blk, blk, g_send, g_recv.at[k * 32 + u2, f2], dev).start()
 
@@ -303,18 +308,18 @@
                 x_ref[c, at, :] = res[8 * c : 8 * c + 8]
 
     ready = []
-    for f2 in range(2):
-        pass_on(u, f2, FIRST[f2])
-    for f2, dz, dx, targets in GATHER:
-        u2 = source(dz, dx)
+    for tree in range(2):
+        pass_on(u, (tree + yh) % 2, FIRST[tree])
+    for tree, dz, dx, targets, over_y in GATHER:
+        u2, f2 = source(dz, dx), (tree + yh) % 2
         if targets is None:
             ready.append(u2)
-            if len(ready) == 2:
+            if len(ready) == 4:
                 cross(*ready)
                 ready = []
         else:
             arrived(k, u2, f2)
-            pass_on(u2, f2, targets)
+            pass_on(u2, f2, targets, over_y)
     most_g = g_ref.at[pl.ds(0, NJ - 1)]
     remote(most_g, most_g, g_send, a_recv, ring_y[0]).wait_send()
     some_a.wait_send()

time: 56.6 us -> 55.8 us (0.986)
  Pallas kernels: 56.4 us -> 55.6 us
    pallas_call x1, Pallas kernels: 52.5 us -> 51.7 us  [body(): pl.pallas_call(exchange_kernel, out_shape=pltpu.VMEM((16, 256, 128), F32)...]
where the time goes in v6:
time: 55.8 us; the launch traced here: 55.7 us
  Pallas kernels  55.6 us (100%)
    pallas_call x1, Pallas kernels, body(): pl.pallas_call(exchange_kernel, out_shape=pltpu.VMEM((16, 256, 128), F32)...  51.7 us
    pallas_call x1, Pallas kernels, body(): pl.pallas_call(output_kernel, out_shape=jax.ShapeDtypeStruct((2048, LAGS)...  3.91 us

profile of v6, /device:TPU:1, one launch (start us, length us, event | category | flops | bytes accessed | tf_op | source)
XLA Modules:
  0.0 55.7 jit_solution(991183049472279116)
XLA Ops:
  0.0 0.0 copy-start
  0.0 0.0 copy-start.1
  0.0 51.7 %exchange.1.x_ref = f32[16,256,128]{2,1,0:T(8,128)S(1)} custom-call(s32[256]{0:T(256)} %idx_hbm.1, f32[256,1024]{1,0:T(8,128)} %bitcast.2, bf16[256,1024]{1,0:T(8,128)(2,1)} %constant.8.clone.hi_hbm, bf16[256,1024]{1,0:T(8,128)(2,1)} %constant.9.clone.lo_hbm), custom_call_target="tpu_custom_call" | custom-call | tf_op jit(solution)/shard_map/exchange/pallas_call | solution.py:362
  51.7 0.0 copy-done
  51.7 0.0 copy-done.1
  51.8 3.9 %correlate.1 = f32[2048,512]{1,0:T(8,128)} custom-call(f32[16,256,128]{2,1,0:T(8,128)S(1)} %exchange.1.x_ref, bf16[256,512]{1,0:T(8,128)(2,1)S(1)} %copy-done.1, bf16[256,512]{1,0:T(8,128)(2,1)S(1)} %copy-done), custom_call_target="tpu_custom_call" | custom-call | tf_op jit(solution)/shard_map/correlate/pallas_call | solution.py:387
Async XLA Ops:
  0.0 51.7 %copy-start = (bf16[256,512]{1,0:T(8,128)(2,1)S(1)}, bf16[256,512]{1,0:T(8,128)(2,1)}, u32[]{:S(2)}) copy-start(bf16[256,512]{1,0:T(8,128)(2,1)} %constant.11.clone.lo_hbm) | copy-start | bytes 786436
  0.0 51.7 %copy-start.1 = (bf16[256,512]{1,0:T(8,128)(2,1)S(1)}, bf16[256,512]{1,0:T(8,128)(2,1)}, u32[]{:S(2)}) copy-start(bf16[256,512]{1,0:T(8,128)(2,1)} %constant.10.clone.hi_hbm) | copy-start | bytes 786436

commit v7 on v6

--- a/solution.py
+++ b/solution.py
@@ -56,7 +56,7 @@
     return lax.dot_general(a, b, (((ca,), (cb,)), ((), ())), preferred_element_type=F32)
 
 
-OFF_Z = (1, -1, 2, -2, 3, -3, 4)
+OFF_Z = (4, 3, -3, 2, -2, 1, -1)
 FIRST = (
     ((-1, 0), (2, 0), (0, -2), (4, 0)),
     ((0, 1), (0, -1), (2, 0)),
@@ -184,7 +184,7 @@
             src_ref=src, dst_ref=dst, send_sem=ssem, recv_sem=rsem, device_id=dev, device_id_type=MESH
         )
 
-    plane = [(xat(d), kk) for d in (0, 1, -1, 2) for kk in (k, 1 - k)][1:]
+    plane = [(xat(d), kk) for d in (2, 1, -1, 0) for kk in (1 - k, k)][:-1]
     ring_y = [(h, (1 - yh) * NJ + s % NJ), (1 - h, s), (1 - h, (1 - yh) * NJ + s % NJ)]
     barrier = pltpu.get_barrier_semaphore()
     for dev in [device(zat(d), x, k) for d in OFF_Z] + [device(z, *p) for p in plane] + ring_y:

time: 55.8 us -> 54.2 us (0.971)
  Pallas kernels: 55.6 us -> 54 us
    pallas_call x1, Pallas kernels: 51.7 us -> 50.1 us  [body(): pl.pallas_call(exchange_kernel, out_shape=pltpu.VMEM((16, 256, 128), F32)...]
where the time goes in v7:
time: 54.2 us; the launch traced here: 54.1 us
  Pallas kernels  54 us (100%)
    pallas_call x1, Pallas kernels, body(): pl.pallas_call(exchange_kernel, out_shape=pltpu.VMEM((16, 256, 128), F32)...  50.1 us
    pallas_call x1, Pallas kernels, body(): pl.pallas_call(output_kernel, out_shape=jax.ShapeDtypeStruct((2048, LAGS)...  3.91 us

profile of v7, /device:TPU:1, one launch (start us, length us, event | category | flops | bytes accessed | tf_op | source)
XLA Modules:
  0.0 54.1 jit_solution(4247847634788717981)
XLA Ops:
  0.0 0.0 copy-start
  0.0 0.0 copy-start.1
  0.0 50.1 %exchange.1.x_ref = f32[16,256,128]{2,1,0:T(8,128)S(1)} custom-call(s32[256]{0:T(256)} %idx_hbm.1, f32[256,1024]{1,0:T(8,128)} %bitcast.2, bf16[256,1024]{1,0:T(8,128)(2,1)} %constant.8.clone.hi_hbm, bf16[256,1024]{1,0:T(8,128)(2,1)} %constant.9.clone.lo_hbm), custom_call_target="tpu_custom_call" | custom-call | tf_op jit(solution)/shard_map/exchange/pallas_call | solution.py:362
  50.1 0.0 copy-done
  50.2 0.0 copy-done.1
  50.2 3.9 %correlate.1 = f32[2048,512]{1,0:T(8,128)} custom-call(f32[16,256,128]{2,1,0:T(8,128)S(1)} %exchange.1.x_ref, bf16[256,512]{1,0:T(8,128)(2,1)S(1)} %copy-done.1, bf16[256,512]{1,0:T(8,128)(2,1)S(1)} %copy-done), custom_call_target="tpu_custom_call" | custom-call | tf_op jit(solution)/shard_map/correlate/pallas_call | solution.py:387
Async XLA Ops:
  0.0 50.1 %copy-start = (bf16[256,512]{1,0:T(8,128)(2,1)S(1)}, bf16[256,512]{1,0:T(8,128)(2,1)}, u32[]{:S(2)}) copy-start(bf16[256,512]{1,0:T(8,128)(2,1)} %constant.11.clone.lo_hbm) | copy-start | bytes 786436
  0.0 50.2 %copy-start.1 = (bf16[256,512]{1,0:T(8,128)(2,1)S(1)}, bf16[256,512]{1,0:T(8,128)(2,1)}, u32[]{:S(2)}) copy-start(bf16[256,512]{1,0:T(8,128)(2,1)} %constant.10.clone.hi_hbm) | copy-start | bytes 786436

commit v8 on v7

--- a/solution.py
+++ b/solution.py
@@ -238,7 +238,7 @@
         remote(pick_ref.at[0], y_ref.at[1], y_send.at[1], y_recv.at[1], ring_y[1]),
         remote(pick_ref.at[0], y_ref.at[2], y_send.at[2], y_recv.at[2], ring_y[2]),
     ]
-    for own in range(2):
+    for own in (1, 0):
         base = (h if own else 1 - h) * 128
 
         def pick(i, carry):

time: 54.2 us -> 54.1 us (level)
  no operation moved by 1% of the time
where the time goes in v8:
time: 54.1 us; the launch traced here: 54 us
  Pallas kernels  54 us (100%)
    pallas_call x1, Pallas kernels, body(): pl.pallas_call(exchange_kernel, out_shape=pltpu.VMEM((16, 256, 128), F32)...  50.1 us
    pallas_call x1, Pallas kernels, body(): pl.pallas_call(output_kernel, out_shape=jax.ShapeDtypeStruct((2048, LAGS)...  3.91 us

profile of v8, /device:TPU:1, one launch (start us, length us, event | category | flops | bytes accessed | tf_op | source)
XLA Modules:
  0.0 54.0 jit_solution(5712422536068742091)
XLA Ops:
  0.0 0.0 copy-start
  0.0 0.0 copy-start.1
  0.0 50.1 %exchange.1.x_ref = f32[16,256,128]{2,1,0:T(8,128)S(1)} custom-call(s32[256]{0:T(256)} %idx_hbm.1, f32[256,1024]{1,0:T(8,128)} %bitcast.2, bf16[256,1024]{1,0:T(8,128)(2,1)} %constant.8.clone.hi_hbm, bf16[256,1024]{1,0:T(8,128)(2,1)} %constant.9.clone.lo_hbm), custom_call_target="tpu_custom_call" | custom-call | tf_op jit(solution)/shard_map/exchange/pallas_call | solution.py:362
  50.1 0.0 copy-done
  50.1 0.0 copy-done.1
  50.1 3.9 %correlate.1 = f32[2048,512]{1,0:T(8,128)} custom-call(f32[16,256,128]{2,1,0:T(8,128)S(1)} %exchange.1.x_ref, bf16[256,512]{1,0:T(8,128)(2,1)S(1)} %copy-done.1, bf16[256,512]{1,0:T(8,128)(2,1)S(1)} %copy-done), custom_call_target="tpu_custom_call" | custom-call | tf_op jit(solution)/shard_map/correlate/pallas_call | solution.py:387
Async XLA Ops:
  0.0 50.1 %copy-start = (bf16[256,512]{1,0:T(8,128)(2,1)S(1)}, bf16[256,512]{1,0:T(8,128)(2,1)}, u32[]{:S(2)}) copy-start(bf16[256,512]{1,0:T(8,128)(2,1)} %constant.11.clone.lo_hbm) | copy-start | bytes 786436
  0.0 50.1 %copy-start.1 = (bf16[256,512]{1,0:T(8,128)(2,1)S(1)}, bf16[256,512]{1,0:T(8,128)(2,1)}, u32[]{:S(2)}) copy-start(bf16[256,512]{1,0:T(8,128)(2,1)} %constant.10.clone.hi_hbm) | copy-start | bytes 786436

commit v9 on v8

--- a/solution.py
+++ b/solution.py
@@ -249,7 +249,7 @@
             gm_ref[own, pl.ds(pl.multiple_of(8 * i, 8), 8), :] = v
             return carry
 
-        lax.fori_loop(0, 128, pick, 0, unroll=16)
+        lax.fori_loop(0, 128, pick, 0, unroll=32)
         got = []
         for t in range(8):
             v = gm_ref[own, 128 * t : 128 * (t + 1), :]
@@ -308,7 +308,7 @@
                 x_ref[c, at, :] = res[8 * c : 8 * c + 8]
 
     ready = []
-    for tree in range(2):
+    for tree in (1, 0):
         pass_on(u, (tree + yh) % 2, FIRST[tree])
     for tree, dz, dx, targets, over_y in GATHER:
         u2, f2 = source(dz, dx), (tree + yh) % 2

time: 54.1 us -> 54.6 us (level)
  no operation moved by 1% of the time
where the time goes in v9:
time: 54.6 us; the launch traced here: 54.5 us
  Pallas kernels  54.4 us (100%)
    pallas_call x1, Pallas kernels, body(): pl.pallas_call(exchange_kernel, out_shape=pltpu.VMEM((16, 256, 128), F32)...  50.5 us
    pallas_call x1, Pallas kernels, body(): pl.pallas_call(output_kernel, out_shape=jax.ShapeDtypeStruct((2048, LAGS)...  3.91 us

profile of v9, /device:TPU:1, one launch (start us, length us, event | category | flops | bytes accessed | tf_op | source)
XLA Modules:
  0.0 54.5 jit_solution(4986037424225957761)
XLA Ops:
  0.0 0.0 copy-start
  0.0 0.0 copy-start.1
  0.0 50.5 %exchange.1.x_ref = f32[16,256,128]{2,1,0:T(8,128)S(1)} custom-call(s32[256]{0:T(256)} %idx_hbm.1, f32[256,1024]{1,0:T(8,128)} %bitcast.2, bf16[256,1024]{1,0:T(8,128)(2,1)} %constant.8.clone.hi_hbm, bf16[256,1024]{1,0:T(8,128)(2,1)} %constant.9.clone.lo_hbm), custom_call_target="tpu_custom_call" | custom-call | tf_op jit(solution)/shard_map/exchange/pallas_call | solution.py:362
  50.5 0.0 copy-done
  50.5 0.0 copy-done.1
  50.5 3.9 %correlate.1 = f32[2048,512]{1,0:T(8,128)} custom-call(f32[16,256,128]{2,1,0:T(8,128)S(1)} %exchange.1.x_ref, bf16[256,512]{1,0:T(8,128)(2,1)S(1)} %copy-done.1, bf16[256,512]{1,0:T(8,128)(2,1)S(1)} %copy-done), custom_call_target="tpu_custom_call" | custom-call | tf_op jit(solution)/shard_map/correlate/pallas_call | solution.py:387
Async XLA Ops:
  0.0 50.5 %copy-start = (bf16[256,512]{1,0:T(8,128)(2,1)S(1)}, bf16[256,512]{1,0:T(8,128)(2,1)}, u32[]{:S(2)}) copy-start(bf16[256,512]{1,0:T(8,128)(2,1)} %constant.11.clone.lo_hbm) | copy-start | bytes 786436
  0.0 50.5 %copy-start.1 = (bf16[256,512]{1,0:T(8,128)(2,1)S(1)}, bf16[256,512]{1,0:T(8,128)(2,1)}, u32[]{:S(2)}) copy-start(bf16[256,512]{1,0:T(8,128)(2,1)} %constant.10.clone.hi_hbm) | copy-start | bytes 786436
